TPU v7x, 512 devices: a whole 4x8x8 slice. The times are simulated.
512 devices in a mesh: seq: 64 (over z, x, core), head: 8 (over y).
Axes of the slice: x: 4, y: 8, z: 8, core: 2. Of those that a mesh axis runs over, the one named last changes fastest.
Arguments:
- queries: bfloat16 [24576, 5120], P(('seq', 'head')), may hold values from -6 to 6
- keys: bfloat16 [24576, 1024], P(('seq', 'head')), may hold values from -6 to 6
- values: bfloat16 [24576, 1024], P(('seq', 'head')), may hold values from -6 to 6
- outputs: bfloat16 [24576, 5120], P(('seq', 'head')), may hold values from -2 to 2
- output_gradient: bfloat16 [24576, 5120], P(('seq', 'head')), may hold values from -6 to 6
- lse: bfloat16 [24576, 40], P(('seq', 'head'))
- ranks: int32 [24576], P(('seq', 'head')), may hold values from 0 to 8192, as said below
Outputs:
- query_grads: bfloat16 [24576, 5120], P(('seq', 'head'))
- key_gradient_output: bfloat16 [24576, 1024], P(('seq', 'head'))
- value_gradient: bfloat16 [24576, 1024], P(('seq', 'head'))
Inputs may be any that keep to these rules, and one draw needn't show every extreme that they name: Home shard s holds slots s * 384 to (s + 1) * 384 - 1. Its live slots are its first c_s slots, with 1 <= c_s <= 384, holding the consecutive ranks P_s, P_s + 1, ..., where P_s is the number of survivors of the shards before s; its other slots hold 8192. One shard holds exactly 384 survivors; all shards together 8192.
All inputs are finite; a program needn't handle non-finite values.
Results may differ from a plain program's by a relative error of at most 0.0056.
Values may be sent and summed in bfloat16 or wider, within the bound.
A program may use at most 64 MiB of HBM per device.

v0:
```python
import jax
import jax.numpy as jnp
from jax import lax
from jax.sharding import PartitionSpec as P

QUERY_HEADS = 40
KEY_VALUE_HEADS = 8
HEAD_SIZE = 128
BALANCED_TOKENS = 128


block_keys = 512


def per_device(queries, keys, values, outputs, output_gradient, lse, ranks):
    sequence_count = lax.axis_size("seq")
    head_total = lax.axis_size("head")
    home_rows = queries.shape[0]
    capacity = home_rows * head_total
    slots = capacity // sequence_count
    surviving_tokens = BALANCED_TOKENS * sequence_count
    group_size = QUERY_HEADS // KEY_VALUE_HEADS
    local_key_value = KEY_VALUE_HEADS // head_total
    scale = HEAD_SIZE ** (-0.5)

    def split_heads(array):
        return array.reshape(home_rows, head_total, array.shape[1] // head_total)

    moved = (
        lax.all_to_all(split_heads(queries), "head", split_axis=1, concat_axis=0, tiled=True),
        lax.all_to_all(split_heads(keys), "head", split_axis=1, concat_axis=0, tiled=True),
        lax.all_to_all(split_heads(values), "head", split_axis=1, concat_axis=0, tiled=True),
        lax.all_to_all(
            split_heads(output_gradient), "head", split_axis=1, concat_axis=0, tiled=True
        ),
        lax.all_to_all(split_heads(lse), "head", split_axis=1, concat_axis=0, tiled=True),
        lax.all_to_all(split_heads(outputs), "head", split_axis=1, concat_axis=0, tiled=True),
    )
    shard_rank_list = lax.all_gather(ranks, "head", axis=0, tiled=True)
    first_rank = shard_rank_list[0]
    living_count = jnp.sum((shard_rank_list < surviving_tokens).astype(jnp.int32))
    table = lax.all_gather(
        jnp.stack([first_rank, living_count])[None, :], "seq", axis=0, tiled=True
    )

    def to_pairs(array):
        flat = array.reshape(slots, sequence_count, array.shape[-1])
        return jnp.roll(flat, first_rank, axis=1)

    arrived = (
        lax.all_to_all(to_pairs(moved[0]), "seq", split_axis=1, concat_axis=1, tiled=True),
        lax.all_to_all(to_pairs(moved[1]), "seq", split_axis=1, concat_axis=1, tiled=True),
        lax.all_to_all(to_pairs(moved[2]), "seq", split_axis=1, concat_axis=1, tiled=True),
        lax.all_to_all(to_pairs(moved[3]), "seq", split_axis=1, concat_axis=1, tiled=True),
        lax.all_to_all(to_pairs(moved[4]), "seq", split_axis=1, concat_axis=1, tiled=True),
        lax.all_to_all(to_pairs(moved[5]), "seq", split_axis=1, concat_axis=1, tiled=True),
    )
    my_index = lax.axis_index("seq")
    starts = table[:, 0]
    count_table = table[:, 1]
    offset = (my_index - starts) % sequence_count
    within = jnp.arange(slots, dtype=jnp.int32)[:, None] * sequence_count + offset[None, :]
    alive = within < count_table[None, :]
    target_rank = jnp.where(
        alive, (starts[None, :] + within) // sequence_count, BALANCED_TOKENS
    ).reshape(-1)

    def place(array):
        width = array.shape[-1]
        return (
            jnp.zeros((BALANCED_TOKENS, width), array.dtype)
            .at[target_rank]
            .set(array.reshape(slots * sequence_count, width), mode="drop")
        )

    query_row_block = place(arrived[0]).reshape(
        BALANCED_TOKENS, local_key_value, group_size, HEAD_SIZE
    )
    key_row_block = place(arrived[1]).reshape(BALANCED_TOKENS, local_key_value, HEAD_SIZE)
    value_row_block = place(arrived[2]).reshape(BALANCED_TOKENS, local_key_value, HEAD_SIZE)
    grad_rows = place(arrived[3]).reshape(BALANCED_TOKENS, local_key_value, group_size, HEAD_SIZE)
    lse_rows = (
        place(arrived[4]).astype(jnp.float32).reshape(BALANCED_TOKENS, local_key_value, group_size)
    )
    out_rows = (
        place(arrived[5])
        .astype(jnp.float32)
        .reshape(BALANCED_TOKENS, local_key_value, group_size, HEAD_SIZE)
    )
    delta_rows = (
        jnp.sum(grad_rows.astype(jnp.float32) * out_rows, axis=-1)
        .astype(jnp.bfloat16)
        .astype(jnp.float32)
    )
    gathered = (
        lax.all_gather(key_row_block, "seq", axis=0, tiled=True),
        lax.all_gather(value_row_block, "seq", axis=0, tiled=True),
    )
    all_keys = gathered[0].reshape(sequence_count, BALANCED_TOKENS, local_key_value, HEAD_SIZE)
    all_values = gathered[1].reshape(sequence_count, BALANCED_TOKENS, local_key_value, HEAD_SIZE)
    rows_per = block_keys // sequence_count
    inner = 1
    outer = BALANCED_TOKENS // rows_per // inner
    query_rank = jnp.arange(BALANCED_TOKENS, dtype=jnp.int32) * sequence_count + my_index
    lse_t = lse_rows.transpose(1, 2, 0)
    delta_t = delta_rows.transpose(1, 2, 0)
    position = jnp.arange(sequence_count * rows_per, dtype=jnp.int32)

    def key_step(query_acc, row_start):
        key_blk = lax.dynamic_slice_in_dim(all_keys, row_start, rows_per, 1).reshape(
            sequence_count * rows_per, local_key_value, HEAD_SIZE
        )
        value_blk = lax.dynamic_slice_in_dim(all_values, row_start, rows_per, 1).reshape(
            sequence_count * rows_per, local_key_value, HEAD_SIZE
        )
        key_owner_rank = (row_start + position % rows_per) * sequence_count + position // rows_per
        mask = key_owner_rank[None, None, None, :] <= query_rank[None, None, :, None]
        scores = (
            jnp.einsum(
                "rgmc,kgc->gmrk", query_row_block, key_blk, preferred_element_type=jnp.float32
            )
            * scale
        )
        probs = jnp.where(mask, jnp.exp(scores - lse_t[..., None]), 0.0)
        dprob = jnp.einsum(
            "rgmc,kgc->gmrk", grad_rows, value_blk, preferred_element_type=jnp.float32
        )
        dscore = probs * (dprob - delta_t[..., None])
        probs_low = probs.astype(jnp.bfloat16)
        dscore_low = dscore.astype(jnp.bfloat16)
        query_acc = query_acc + scale * jnp.einsum(
            "gmrk,kgc->rgmc", dscore_low, key_blk, preferred_element_type=jnp.float32
        )
        key_part = scale * jnp.einsum(
            "gmrk,rgmc->kgc", dscore_low, query_row_block, preferred_element_type=jnp.float32
        )
        value_part = jnp.einsum(
            "gmrk,rgmc->kgc", probs_low, grad_rows, preferred_element_type=jnp.float32
        )
        return (
            query_acc,
            key_part.reshape(sequence_count, rows_per, local_key_value * HEAD_SIZE),
            value_part.reshape(sequence_count, rows_per, local_key_value * HEAD_SIZE),
        )

    def outer_step(query_acc, outer_index):

        def inner_step(query_inner, inner_index):
            row_start = (outer_index * inner + inner_index) * rows_per
            query_new, key_part, value_part = key_step(query_inner, row_start)
            return (query_new, (key_part, value_part))

        query_acc, (key_parts, value_parts) = lax.scan(
            inner_step, query_acc, jnp.arange(inner, dtype=jnp.int32)
        )
        key_parts = key_parts.transpose(1, 0, 2, 3).reshape(
            sequence_count, inner * rows_per, local_key_value * HEAD_SIZE
        )
        value_parts = value_parts.transpose(1, 0, 2, 3).reshape(
            sequence_count, inner * rows_per, local_key_value * HEAD_SIZE
        )
        received = (
            lax.all_to_all(key_parts, "seq", split_axis=0, concat_axis=0, tiled=True),
            lax.all_to_all(value_parts, "seq", split_axis=0, concat_axis=0, tiled=True),
        )
        return (query_acc, (jnp.sum(received[0], axis=0), jnp.sum(received[1], axis=0)))

    start_acc = jnp.zeros((BALANCED_TOKENS, local_key_value, group_size, HEAD_SIZE), jnp.float32)
    query_acc, (key_sums, value_sums) = lax.scan(
        outer_step, start_acc, jnp.arange(outer, dtype=jnp.int32)
    )
    query_done = query_acc.reshape(
        BALANCED_TOKENS, local_key_value * group_size * HEAD_SIZE
    ).astype(jnp.bfloat16)
    key_done = key_sums.reshape(BALANCED_TOKENS, local_key_value * HEAD_SIZE).astype(jnp.bfloat16)
    value_done = value_sums.reshape(BALANCED_TOKENS, local_key_value * HEAD_SIZE).astype(
        jnp.bfloat16
    )
    safe_rows = jnp.minimum(target_rank, BALANCED_TOKENS - 1)
    alive_flat = alive.reshape(-1)

    def collect(array):
        picked = jnp.where(alive_flat[:, None], array[safe_rows], jnp.zeros((), array.dtype))
        return picked.reshape(slots, sequence_count, array.shape[-1])

    returned = (
        lax.all_to_all(collect(query_done), "seq", split_axis=1, concat_axis=1, tiled=True),
        lax.all_to_all(collect(key_done), "seq", split_axis=1, concat_axis=1, tiled=True),
        lax.all_to_all(collect(value_done), "seq", split_axis=1, concat_axis=1, tiled=True),
    )

    def to_home(array):
        unrolled = jnp.roll(array, -first_rank, axis=1)
        return unrolled.reshape(capacity, 1, array.shape[-1])

    homed = (
        lax.all_to_all(to_home(returned[0]), "head", split_axis=0, concat_axis=1, tiled=True),
        lax.all_to_all(to_home(returned[1]), "head", split_axis=0, concat_axis=1, tiled=True),
        lax.all_to_all(to_home(returned[2]), "head", split_axis=0, concat_axis=1, tiled=True),
    )
    query_grads = homed[0].reshape(home_rows, head_total * homed[0].shape[-1])
    key_gradient_output = homed[1].reshape(home_rows, head_total * homed[1].shape[-1])
    value_gradient = homed[2].reshape(home_rows, head_total * homed[2].shape[-1])
    return (query_grads, key_gradient_output, value_gradient)


def solution(mesh):
    placed = (
        P(("seq", "head"), None),
        P(("seq", "head"), None),
        P(("seq", "head"), None),
        P(("seq", "head"), None),
        P(("seq", "head"), None),
        P(("seq", "head"), None),
        P(("seq", "head")),
    )
    return jax.shard_map(
        per_device,
        mesh=mesh,
        in_specs=placed,
        out_specs=(P(("seq", "head"), None), P(("seq", "head"), None), P(("seq", "head"), None)),
        check_vma=False,
    )
```

profile of v0, /device:TPU:1, one launch (start us, length us, event | category | flops | bytes accessed | tf_op | source)
XLA Modules:
  0.0 1037.1 jit_solution(14550851297017344415)
XLA Ops:
  10.1 12.0 %all-reduce = s32[384]{0:T(512)S(1)} all-reduce(s32[384]{0:T(512)S(1)} %dynamic-update-slice), channel_id=1, replica_groups=mesh['seq'=64,'head'=8] {'head'}, use_global_device_ids=true, to_apply=%add | all-reduce | flops 384 | bytes 3072
  28.5 25.6 %all-reduce.1 = s32[128]{0:T(128)S(1)} all-reduce(s32[128]{0:T(128)S(1)} %add_dynamic-update-slice_fusion), channel_id=2, replica_groups=mesh['seq'=64,'head'=8] {'seq'}, use_global_device_ids=true, to_apply=%add.1 | all-reduce | flops 128 | bytes 1024
  77.4 11.0 %all-to-all-done.3 = bf16[6,64,128]{2,0,1:T(8,128)(2,1)S(1)} async-done(((bf16[6,64,128]{2,0,1:T(8,128)(2,1)}), bf16[6,64,128]{2,0,1:T(8,128)(2,1)S(1)}, u32[]{:S(2)}, u32[]{:S(2)}) %all-to-all-start.3) | async-done | bytes 98336 | tf_op jit(solution)/shard_map/all_to_all | solution.py:52
  135.2 11.1 %all-to-all-done.9 = bf16[6,64,128]{2,0,1:T(8,128)(2,1)S(1)} async-done(((bf16[6,64,128]{2,0,1:T(8,128)(2,1)}), bf16[6,64,128]{2,0,1:T(8,128)(2,1)S(1)}, u32[]{:S(2)}, u32[]{:S(2)}) %all-to-all-start.9) | async-done | bytes 98336 | tf_op jit(solution)/shard_map/all_to_all | solution.py:53
  150.7 16.3 %all-to-all-done.4 = bf16[48,8,640]{2,0,1:T(8,128)(2,1)S(1)} async-done(((bf16[48,8,640]{2,0,1:T(8,128)(2,1)}), bf16[48,8,640]{2,0,1:T(8,128)(2,1)S(1)}, u32[]{:S(2)}, u32[]{:S(2)}) %all-to-all-start.4) | async-done | bytes 491552 | tf_op jit(solution)/shard_map/all_to_all | solution.py:30
  173.4 14.2 %all-to-all-done.12 = bf16[48,8,640]{2,0,1:T(8,128)(2,1)S(1)} async-done(((bf16[48,8,640]{2,0,1:T(8,128)(2,1)}), bf16[48,8,640]{2,0,1:T(8,128)(2,1)S(1)}, u32[]{:S(2)}, u32[]{:S(2)}) %all-to-all-start.12) | async-done | bytes 491552 | tf_op jit(solution)/shard_map/all_to_all | solution.py:37
  192.7 15.7 %all-to-all-done.10 = bf16[48,8,640]{2,0,1:T(8,128)(2,1)S(1)} async-done(((bf16[48,8,640]{2,0,1:T(8,128)(2,1)}), bf16[48,8,640]{2,0,1:T(8,128)(2,1)S(1)}, u32[]{:S(2)}, u32[]{:S(2)}) %all-to-all-start.10) | async-done | bytes 491552 | tf_op jit(solution)/shard_map/all_to_all | solution.py:33
  214.4 19.8 %all-to-all-done.5 = bf16[6,64,640]{2,0,1:T(8,128)(2,1)S(1)} async-done(((bf16[6,64,640]{2,0,1:T(8,128)(2,1)}), bf16[6,64,640]{2,0,1:T(8,128)(2,1)S(1)}, u32[]{:S(2)}, u32[]{:S(2)}) %all-to-all-start.5) | async-done | bytes 491552 | tf_op jit(solution)/shard_map/all_to_all | solution.py:51
  241.4 19.7 %all-to-all-done.13 = bf16[6,64,640]{2,0,1:T(8,128)(2,1)S(1)} async-done(((bf16[6,64,640]{2,0,1:T(8,128)(2,1)}), bf16[6,64,640]{2,0,1:T(8,128)(2,1)S(1)}, u32[]{:S(2)}, u32[]{:S(2)}) %all-to-all-start.13) | async-done | bytes 491552 | tf_op jit(solution)/shard_map/all_to_all | solution.py:56
  274.3 13.1 %all-to-all-done.11 = bf16[6,64,640]{2,0,1:T(8,128)(2,1)S(1)} async-done(((bf16[6,64,640]{2,0,1:T(8,128)(2,1)}), bf16[6,64,640]{2,0,1:T(8,128)(2,1)S(1)}, u32[]{:S(2)}, u32[]{:S(2)}) %all-to-all-start.11) | async-done | bytes 491552 | tf_op jit(solution)/shard_map/all_to_all | solution.py:54
  290.3 635.0 %while.26 = (s32[]{:T(128)}, f32[128,1,5,128]{0,3,2,1:T(8,128)S(1)}, bf16[16,8,128]{2,1,0:T(8,128)(2,1)S(1)}, bf16[16,8,128]{2,1,0:T(8,128)(2,1)S(1)}, s32[16]{0...) while((s32[]{:T(128)}, ...), condition=%wide.region_11.14_spmd.clone.clone, body=%wide.region_8.13_spmd.clone.clone.sunk | while | flops 422237952 | bytes 10378573 | solution.py:169
  319.2 11.7 %all-to-all-done = f32[64,8,128]{2,1,0:T(8,128)S(1)} async-done(((f32[64,8,128]{2,1,0:T(8,128)}), f32[64,8,128]{2,1,0:T(8,128)S(1)}, u32[]{:S(2)}, u32[]{:S(2)}) %all-to-all-start) | async-done | bytes 262176 | tf_op jit(solution)/shard_map/while/body/eval_jaxpr/all_to_all | solution.py:163
  358.8 11.7 %all-to-all-done = f32[64,8,128]{2,1,0:T(8,128)S(1)} async-done(((f32[64,8,128]{2,1,0:T(8,128)}), f32[64,8,128]{2,1,0:T(8,128)S(1)}, u32[]{:S(2)}, u32[]{:S(2)}) %all-to-all-start) | async-done | bytes 262176 | tf_op jit(solution)/shard_map/while/body/eval_jaxpr/all_to_all | solution.py:163
  381.5 10.8 %all-to-all-done.1 = f32[64,8,128]{2,1,0:T(8,128)S(1)} async-done(((f32[64,8,128]{2,1,0:T(8,128)}), f32[64,8,128]{2,1,0:T(8,128)S(1)}, u32[]{:S(2)}, u32[]{:S(2)}) %all-to-all-start.1) | async-done | bytes 262176 | tf_op jit(solution)/shard_map/while/body/eval_jaxpr/all_to_all | solution.py:164
  398.5 11.7 %all-to-all-done = f32[64,8,128]{2,1,0:T(8,128)S(1)} async-done(((f32[64,8,128]{2,1,0:T(8,128)}), f32[64,8,128]{2,1,0:T(8,128)S(1)}, u32[]{:S(2)}, u32[]{:S(2)}) %all-to-all-start) | async-done | bytes 262176 | tf_op jit(solution)/shard_map/while/body/eval_jaxpr/all_to_all | solution.py:163
  438.1 11.7 %all-to-all-done = f32[64,8,128]{2,1,0:T(8,128)S(1)} async-done(((f32[64,8,128]{2,1,0:T(8,128)}), f32[64,8,128]{2,1,0:T(8,128)S(1)}, u32[]{:S(2)}, u32[]{:S(2)}) %all-to-all-start) | async-done | bytes 262176 | tf_op jit(solution)/shard_map/while/body/eval_jaxpr/all_to_all | solution.py:163
  477.7 11.7 %all-to-all-done = f32[64,8,128]{2,1,0:T(8,128)S(1)} async-done(((f32[64,8,128]{2,1,0:T(8,128)}), f32[64,8,128]{2,1,0:T(8,128)S(1)}, u32[]{:S(2)}, u32[]{:S(2)}) %all-to-all-start) | async-done | bytes 262176 | tf_op jit(solution)/shard_map/while/body/eval_jaxpr/all_to_all | solution.py:163
  517.3 11.7 %all-to-all-done = f32[64,8,128]{2,1,0:T(8,128)S(1)} async-done(((f32[64,8,128]{2,1,0:T(8,128)}), f32[64,8,128]{2,1,0:T(8,128)S(1)}, u32[]{:S(2)}, u32[]{:S(2)}) %all-to-all-start) | async-done | bytes 262176 | tf_op jit(solution)/shard_map/while/body/eval_jaxpr/all_to_all | solution.py:163
  556.9 11.7 %all-to-all-done = f32[64,8,128]{2,1,0:T(8,128)S(1)} async-done(((f32[64,8,128]{2,1,0:T(8,128)}), f32[64,8,128]{2,1,0:T(8,128)S(1)}, u32[]{:S(2)}, u32[]{:S(2)}) %all-to-all-start) | async-done | bytes 262176 | tf_op jit(solution)/shard_map/while/body/eval_jaxpr/all_to_all | solution.py:163
  579.6 10.8 %all-to-all-done.1 = f32[64,8,128]{2,1,0:T(8,128)S(1)} async-done(((f32[64,8,128]{2,1,0:T(8,128)}), f32[64,8,128]{2,1,0:T(8,128)S(1)}, u32[]{:S(2)}, u32[]{:S(2)}) %all-to-all-start.1) | async-done | bytes 262176 | tf_op jit(solution)/shard_map/while/body/eval_jaxpr/all_to_all | solution.py:164
  596.6 11.7 %all-to-all-done = f32[64,8,128]{2,1,0:T(8,128)S(1)} async-done(((f32[64,8,128]{2,1,0:T(8,128)}), f32[64,8,128]{2,1,0:T(8,128)S(1)}, u32[]{:S(2)}, u32[]{:S(2)}) %all-to-all-start) | async-done | bytes 262176 | tf_op jit(solution)/shard_map/while/body/eval_jaxpr/all_to_all | solution.py:163
  636.2 11.7 %all-to-all-done = f32[64,8,128]{2,1,0:T(8,128)S(1)} async-done(((f32[64,8,128]{2,1,0:T(8,128)}), f32[64,8,128]{2,1,0:T(8,128)S(1)}, u32[]{:S(2)}, u32[]{:S(2)}) %all-to-all-start) | async-done | bytes 262176 | tf_op jit(solution)/shard_map/while/body/eval_jaxpr/all_to_all | solution.py:163
  675.8 11.7 %all-to-all-done = f32[64,8,128]{2,1,0:T(8,128)S(1)} async-done(((f32[64,8,128]{2,1,0:T(8,128)}), f32[64,8,128]{2,1,0:T(8,128)S(1)}, u32[]{:S(2)}, u32[]{:S(2)}) %all-to-all-start) | async-done | bytes 262176 | tf_op jit(solution)/shard_map/while/body/eval_jaxpr/all_to_all | solution.py:163
  715.4 11.7 %all-to-all-done = f32[64,8,128]{2,1,0:T(8,128)S(1)} async-done(((f32[64,8,128]{2,1,0:T(8,128)}), f32[64,8,128]{2,1,0:T(8,128)S(1)}, u32[]{:S(2)}, u32[]{:S(2)}) %all-to-all-start) | async-done | bytes 262176 | tf_op jit(solution)/shard_map/while/body/eval_jaxpr/all_to_all | solution.py:163
  755.1 11.7 %all-to-all-done = f32[64,8,128]{2,1,0:T(8,128)S(1)} async-done(((f32[64,8,128]{2,1,0:T(8,128)}), f32[64,8,128]{2,1,0:T(8,128)S(1)}, u32[]{:S(2)}, u32[]{:S(2)}) %all-to-all-start) | async-done | bytes 262176 | tf_op jit(solution)/shard_map/while/body/eval_jaxpr/all_to_all | solution.py:163
  794.7 11.7 %all-to-all-done = f32[64,8,128]{2,1,0:T(8,128)S(1)} async-done(((f32[64,8,128]{2,1,0:T(8,128)}), f32[64,8,128]{2,1,0:T(8,128)S(1)}, u32[]{:S(2)}, u32[]{:S(2)}) %all-to-all-start) | async-done | bytes 262176 | tf_op jit(solution)/shard_map/while/body/eval_jaxpr/all_to_all | solution.py:163
  834.3 11.7 %all-to-all-done = f32[64,8,128]{2,1,0:T(8,128)S(1)} async-done(((f32[64,8,128]{2,1,0:T(8,128)}), f32[64,8,128]{2,1,0:T(8,128)S(1)}, u32[]{:S(2)}, u32[]{:S(2)}) %all-to-all-start) | async-done | bytes 262176 | tf_op jit(solution)/shard_map/while/body/eval_jaxpr/all_to_all | solution.py:163
  873.9 11.7 %all-to-all-done = f32[64,8,128]{2,1,0:T(8,128)S(1)} async-done(((f32[64,8,128]{2,1,0:T(8,128)}), f32[64,8,128]{2,1,0:T(8,128)S(1)}, u32[]{:S(2)}, u32[]{:S(2)}) %all-to-all-start) | async-done | bytes 262176 | tf_op jit(solution)/shard_map/while/body/eval_jaxpr/all_to_all | solution.py:163
  913.5 11.7 %all-to-all-done = f32[64,8,128]{2,1,0:T(8,128)S(1)} async-done(((f32[64,8,128]{2,1,0:T(8,128)}), f32[64,8,128]{2,1,0:T(8,128)S(1)}, u32[]{:S(2)}, u32[]{:S(2)}) %all-to-all-start) | async-done | bytes 262176 | tf_op jit(solution)/shard_map/while/body/eval_jaxpr/all_to_all | solution.py:163
  929.0 15.7 %all_to_all.206 = bf16[6,64,128]{2,0,1:T(8,128)(2,1)S(1)} all-to-all(bf16[6,64,128]{2,0,1:T(8,128)(2,1)S(1)} %get-tuple-element.496), channel_id=1, replica_groups=mesh['seq'=64,'head'=8] {'seq'}, dimensions={1} | all-to-all | bytes 196608 | tf_op jit(solution)/shard_map/all_to_all | solution.py:189
  980.5 19.1 %all-to-all-done.14 = bf16[6,64,640]{2,0,1:T(8,128)(2,1)S(1)} async-done(((bf16[6,64,640]{2,0,1:T(8,128)(2,1)}), bf16[6,64,640]{2,0,1:T(8,128)(2,1)S(1)}, u32[]{:S(2)}, u32[]{:S(2)}) %all-to-all-start.14) | async-done | bytes 491552 | tf_op jit(solution)/shard_map/all_to_all | solution.py:187
  1015.5 13.5 %all-to-all-done.15 = bf16[8,2,15360]{2,1,0:T(2,128)(2,1)S(1)} async-done(((bf16[8,2,15360]{2,1,0:T(2,128)(2,1)}), bf16[8,2,15360]{2,1,0:T(2,128)(2,1)S(1)}, u32[]{:S(2)}, u32[]{:S(2)}) %all-to-all-start.15) | async-done | bytes 491552 | tf_op jit(solution)/shard_map/all_to_all | solution.py:197
  (406 shorter events, 591.2 us)
Async XLA Ops:
  66.8 21.6 %all-to-all-start.3 = ((bf16[6,64,128]{2,0,1:T(8,128)(2,1)}), bf16[6,64,128]{2,0,1:T(8,128)(2,1)S(1)}, u32[]{:S(2)}, u32[]{:S(2)}) async-start(bf16[6,64,128]{2,0,1:T(8,128)(2,1)} %copy.75), calls=%async_computation.3 | async-start | bytes 262144 | tf_op jit(solution)/shard_map/all_to_all | solution.py:52
  77.1 213.2 %all-gather.6.cloned.1.call-start = ((), (), s32[]{:S(2)}) async-start(), calls=%async_computation.20 | async-start | bytes 2129920 | tf_op jit(solution)/shard_map/all_gather | solution.py:96
  111.9 18.1 %all-to-all-start.7 = ((bf16[6,64,5]{0,2,1:T(8,128)(2,1)}), bf16[6,64,5]{0,2,1:T(8,128)(2,1)S(1)}, u32[]{:S(2)}, u32[]{:S(2)}) async-start(bf16[6,64,5]{0,2,1:T(8,128)(2,1)} %copy.82), calls=%async_computation.7 | async-start | bytes 262144 | tf_op jit(solution)/shard_map/all_to_all | solution.py:55
  146.3 20.7 %all-to-all-start.4 = ((bf16[48,8,640]{2,0,1:T(8,128)(2,1)}), bf16[48,8,640]{2,0,1:T(8,128)(2,1)S(1)}, u32[]{:S(2)}, u32[]{:S(2)}) async-start(bf16[48,8,640]{2,0,1:T(8,128)(2,1)} %bitcast.208), calls=%async_computation.4 | async-start | bytes 983040 | tf_op jit(solution)/shard_map/all_to_all | solution.py:30
  167.0 20.7 %all-to-all-start.12 = ((bf16[48,8,640]{2,0,1:T(8,128)(2,1)}), bf16[48,8,640]{2,0,1:T(8,128)(2,1)S(1)}, u32[]{:S(2)}, u32[]{:S(2)}) async-start(bf16[48,8,640]{2,0,1:T(8,128)(2,1)} %bitcast.206), calls=%async_computation.12 | async-start | bytes 983040 | tf_op jit(solution)/shard_map/all_to_all | solution.py:37
  170.5 119.8 %all-gather.8.cloned.1.call-start = ((), (), s32[]{:S(2)}) async-start(), calls=%async_computation.21 | async-start | bytes 2129920 | tf_op jit(solution)/shard_map/all_gather | solution.py:97
  187.7 20.7 %all-to-all-start.10 = ((bf16[48,8,640]{2,0,1:T(8,128)(2,1)}), bf16[48,8,640]{2,0,1:T(8,128)(2,1)S(1)}, u32[]{:S(2)}, u32[]{:S(2)}) async-start(bf16[48,8,640]{2,0,1:T(8,128)(2,1)} %bitcast.207), calls=%async_computation.10 | async-start | bytes 983040 | tf_op jit(solution)/shard_map/all_to_all | solution.py:33
  208.3 25.8 %all-to-all-start.5 = ((bf16[6,64,640]{2,0,1:T(8,128)(2,1)}), bf16[6,64,640]{2,0,1:T(8,128)(2,1)S(1)}, u32[]{:S(2)}, u32[]{:S(2)}) async-start(bf16[6,64,640]{2,0,1:T(8,128)(2,1)} %copy.78), calls=%async_computation.5 | async-start | bytes 1310720 | tf_op jit(solution)/shard_map/all_to_all | solution.py:51
  234.2 26.9 %all-to-all-start.13 = ((bf16[6,64,640]{2,0,1:T(8,128)(2,1)}), bf16[6,64,640]{2,0,1:T(8,128)(2,1)S(1)}, u32[]{:S(2)}, u32[]{:S(2)}) async-start(bf16[6,64,640]{2,0,1:T(8,128)(2,1)} %copy.93), calls=%async_computation.13 | async-start | bytes 1310720 | tf_op jit(solution)/shard_map/all_to_all | solution.py:56
  261.1 26.4 %all-to-all-start.11 = ((bf16[6,64,640]{2,0,1:T(8,128)(2,1)}), bf16[6,64,640]{2,0,1:T(8,128)(2,1)S(1)}, u32[]{:S(2)}, u32[]{:S(2)}) async-start(bf16[6,64,640]{2,0,1:T(8,128)(2,1)} %copy.89), calls=%async_computation.11 | async-start | bytes 1310720 | tf_op jit(solution)/shard_map/all_to_all | solution.py:54
  294.2 18.9 %all-to-all-start.1 = ((f32[64,8,128]{2,1,0:T(8,128)}), f32[64,8,128]{2,1,0:T(8,128)S(1)}, u32[]{:S(2)}, u32[]{:S(2)}) async-start(f32[64,8,128]{2,1,0:T(8,128)} %convolution_bitcast_fusion.4), calls=%async_computation.1 | async-start | bytes 524288 | tf_op jit(solution)/shard_map/while/body/eval_jaxpr/all_to_all | solution.py:164
  313.1 17.9 %all-to-all-start = ((f32[64,8,128]{2,1,0:T(8,128)}), f32[64,8,128]{2,1,0:T(8,128)S(1)}, u32[]{:S(2)}, u32[]{:S(2)}) async-start(f32[64,8,128]{2,1,0:T(8,128)} %fusion.102), calls=%async_computation | async-start | bytes 524288 | tf_op jit(solution)/shard_map/while/body/eval_jaxpr/all_to_all | solution.py:163
  334.8 17.9 %all-to-all-start.1 = ((f32[64,8,128]{2,1,0:T(8,128)}), f32[64,8,128]{2,1,0:T(8,128)S(1)}, u32[]{:S(2)}, u32[]{:S(2)}) async-start(f32[64,8,128]{2,1,0:T(8,128)} %convolution_bitcast_fusion.4), calls=%async_computation.1 | async-start | bytes 524288 | tf_op jit(solution)/shard_map/while/body/eval_jaxpr/all_to_all | solution.py:164
  352.7 17.9 %all-to-all-start = ((f32[64,8,128]{2,1,0:T(8,128)}), f32[64,8,128]{2,1,0:T(8,128)S(1)}, u32[]{:S(2)}, u32[]{:S(2)}) async-start(f32[64,8,128]{2,1,0:T(8,128)} %fusion.102), calls=%async_computation | async-start | bytes 524288 | tf_op jit(solution)/shard_map/while/body/eval_jaxpr/all_to_all | solution.py:163
  374.4 17.9 %all-to-all-start.1 = ((f32[64,8,128]{2,1,0:T(8,128)}), f32[64,8,128]{2,1,0:T(8,128)S(1)}, u32[]{:S(2)}, u32[]{:S(2)}) async-start(f32[64,8,128]{2,1,0:T(8,128)} %convolution_bitcast_fusion.4), calls=%async_computation.1 | async-start | bytes 524288 | tf_op jit(solution)/shard_map/while/body/eval_jaxpr/all_to_all | solution.py:164
  392.3 17.9 %all-to-all-start = ((f32[64,8,128]{2,1,0:T(8,128)}), f32[64,8,128]{2,1,0:T(8,128)S(1)}, u32[]{:S(2)}, u32[]{:S(2)}) async-start(f32[64,8,128]{2,1,0:T(8,128)} %fusion.102), calls=%async_computation | async-start | bytes 524288 | tf_op jit(solution)/shard_map/while/body/eval_jaxpr/all_to_all | solution.py:163
  414.1 17.9 %all-to-all-start.1 = ((f32[64,8,128]{2,1,0:T(8,128)}), f32[64,8,128]{2,1,0:T(8,128)S(1)}, u32[]{:S(2)}, u32[]{:S(2)}) async-start(f32[64,8,128]{2,1,0:T(8,128)} %convolution_bitcast_fusion.4), calls=%async_computation.1 | async-start | bytes 524288 | tf_op jit(solution)/shard_map/while/body/eval_jaxpr/all_to_all | solution.py:164
  431.9 17.9 %all-to-all-start = ((f32[64,8,128]{2,1,0:T(8,128)}), f32[64,8,128]{2,1,0:T(8,128)S(1)}, u32[]{:S(2)}, u32[]{:S(2)}) async-start(f32[64,8,128]{2,1,0:T(8,128)} %fusion.102), calls=%async_computation | async-start | bytes 524288 | tf_op jit(solution)/shard_map/while/body/eval_jaxpr/all_to_all | solution.py:163
  471.5 17.9 %all-to-all-start = ((f32[64,8,128]{2,1,0:T(8,128)}), f32[64,8,128]{2,1,0:T(8,128)S(1)}, u32[]{:S(2)}, u32[]{:S(2)}) async-start(f32[64,8,128]{2,1,0:T(8,128)} %fusion.102), calls=%async_computation | async-start | bytes 524288 | tf_op jit(solution)/shard_map/while/body/eval_jaxpr/all_to_all | solution.py:163
  511.2 17.9 %all-to-all-start = ((f32[64,8,128]{2,1,0:T(8,128)}), f32[64,8,128]{2,1,0:T(8,128)S(1)}, u32[]{:S(2)}, u32[]{:S(2)}) async-start(f32[64,8,128]{2,1,0:T(8,128)} %fusion.102), calls=%async_computation | async-start | bytes 524288 | tf_op jit(solution)/shard_map/while/body/eval_jaxpr/all_to_all | solution.py:163
  550.8 17.9 %all-to-all-start = ((f32[64,8,128]{2,1,0:T(8,128)}), f32[64,8,128]{2,1,0:T(8,128)S(1)}, u32[]{:S(2)}, u32[]{:S(2)}) async-start(f32[64,8,128]{2,1,0:T(8,128)} %fusion.102), calls=%async_computation | async-start | bytes 524288 | tf_op jit(solution)/shard_map/while/body/eval_jaxpr/all_to_all | solution.py:163
  590.4 17.9 %all-to-all-start = ((f32[64,8,128]{2,1,0:T(8,128)}), f32[64,8,128]{2,1,0:T(8,128)S(1)}, u32[]{:S(2)}, u32[]{:S(2)}) async-start(f32[64,8,128]{2,1,0:T(8,128)} %fusion.102), calls=%async_computation | async-start | bytes 524288 | tf_op jit(solution)/shard_map/while/body/eval_jaxpr/all_to_all | solution.py:163
  630.0 17.9 %all-to-all-start = ((f32[64,8,128]{2,1,0:T(8,128)}), f32[64,8,128]{2,1,0:T(8,128)S(1)}, u32[]{:S(2)}, u32[]{:S(2)}) async-start(f32[64,8,128]{2,1,0:T(8,128)} %fusion.102), calls=%async_computation | async-start | bytes 524288 | tf_op jit(solution)/shard_map/while/body/eval_jaxpr/all_to_all | solution.py:163
  669.6 17.9 %all-to-all-start = ((f32[64,8,128]{2,1,0:T(8,128)}), f32[64,8,128]{2,1,0:T(8,128)S(1)}, u32[]{:S(2)}, u32[]{:S(2)}) async-start(f32[64,8,128]{2,1,0:T(8,128)} %fusion.102), calls=%async_computation | async-start | bytes 524288 | tf_op jit(solution)/shard_map/while/body/eval_jaxpr/all_to_all | solution.py:163
  709.3 17.9 %all-to-all-start = ((f32[64,8,128]{2,1,0:T(8,128)}), f32[64,8,128]{2,1,0:T(8,128)S(1)}, u32[]{:S(2)}, u32[]{:S(2)}) async-start(f32[64,8,128]{2,1,0:T(8,128)} %fusion.102), calls=%async_computation | async-start | bytes 524288 | tf_op jit(solution)/shard_map/while/body/eval_jaxpr/all_to_all | solution.py:163
  748.9 17.9 %all-to-all-start = ((f32[64,8,128]{2,1,0:T(8,128)}), f32[64,8,128]{2,1,0:T(8,128)S(1)}, u32[]{:S(2)}, u32[]{:S(2)}) async-start(f32[64,8,128]{2,1,0:T(8,128)} %fusion.102), calls=%async_computation | async-start | bytes 524288 | tf_op jit(solution)/shard_map/while/body/eval_jaxpr/all_to_all | solution.py:163
  788.5 17.9 %all-to-all-start = ((f32[64,8,128]{2,1,0:T(8,128)}), f32[64,8,128]{2,1,0:T(8,128)S(1)}, u32[]{:S(2)}, u32[]{:S(2)}) async-start(f32[64,8,128]{2,1,0:T(8,128)} %fusion.102), calls=%async_computation | async-start | bytes 524288 | tf_op jit(solution)/shard_map/while/body/eval_jaxpr/all_to_all | solution.py:163
  828.1 17.9 %all-to-all-start = ((f32[64,8,128]{2,1,0:T(8,128)}), f32[64,8,128]{2,1,0:T(8,128)S(1)}, u32[]{:S(2)}, u32[]{:S(2)}) async-start(f32[64,8,128]{2,1,0:T(8,128)} %fusion.102), calls=%async_computation | async-start | bytes 524288 | tf_op jit(solution)/shard_map/while/body/eval_jaxpr/all_to_all | solution.py:163
  867.8 17.9 %all-to-all-start = ((f32[64,8,128]{2,1,0:T(8,128)}), f32[64,8,128]{2,1,0:T(8,128)S(1)}, u32[]{:S(2)}, u32[]{:S(2)}) async-start(f32[64,8,128]{2,1,0:T(8,128)} %fusion.102), calls=%async_computation | async-start | bytes 524288 | tf_op jit(solution)/shard_map/while/body/eval_jaxpr/all_to_all | solution.py:163
  907.4 17.9 %all-to-all-start = ((f32[64,8,128]{2,1,0:T(8,128)}), f32[64,8,128]{2,1,0:T(8,128)S(1)}, u32[]{:S(2)}, u32[]{:S(2)}) async-start(f32[64,8,128]{2,1,0:T(8,128)} %fusion.102), calls=%async_computation | async-start | bytes 524288 | tf_op jit(solution)/shard_map/while/body/eval_jaxpr/all_to_all | solution.py:163
  973.3 26.4 %all-to-all-start.14 = ((bf16[6,64,640]{2,0,1:T(8,128)(2,1)}), bf16[6,64,640]{2,0,1:T(8,128)(2,1)S(1)}, u32[]{:S(2)}, u32[]{:S(2)}) async-start(bf16[6,64,640]{2,0,1:T(8,128)(2,1)} %copy_select_fusion), calls=%async_computation.14 | async-start | bytes 1310720 | tf_op jit(solution)/shard_map/all_to_all | solution.py:187
  1010.4 18.6 %all-to-all-start.15 = ((bf16[8,2,15360]{2,1,0:T(2,128)(2,1)}), bf16[8,2,15360]{2,1,0:T(2,128)(2,1)S(1)}, u32[]{:S(2)}, u32[]{:S(2)}) async-start(bf16[8,2,15360]{2,1,0:T(2,128)(2,1)} %reshape.722), calls=%async_computation.15 | async-start | bytes 983040 | tf_op jit(solution)/shard_map/all_to_all | solution.py:197
  (25 other events, 639.8 us)
Sparse Core Ops, SparseCore 0:
  90.6 73.4 all-gather.5
  175.2 80.8 all-gather.7
where the time goes:
time: 1040 us
  waiting for transfers between devices  563 us (54%)
  starting transfers between devices  233 us (22%)
  matrix products  95 us (9%)
  blocking collectives  53.3 us (5%)
  local copies, waits for them, and re-layouts  49.2 us (5%)
  between operations  18.5 us (2%)
  other arithmetic  13.6 us (1%)
  loops' own time  11.9 us (1%)
    all_to_all x16, waiting for transfers between devices, outer_step(): lax.all_to_all(key_parts, 'seq', split_axis=0, concat_axis=0, tiled=True)  187 us
    all_to_all x16, waiting for transfers between devices, outer_step(): lax.all_to_all(value_parts, 'seq', split_axis=0, concat_axis=0, tiled=True)  173 us
    all_to_all x16, starting transfers between devices, outer_step(): lax.all_to_all(value_parts, 'seq', split_axis=0, concat_axis=0, tiled=True)  77.3 us
    all_to_all x16, starting transfers between devices, outer_step(): lax.all_to_all(key_parts, 'seq', split_axis=0, concat_axis=0, tiled=True)  76.4 us
    unnamed x2, blocking collectives  37.6 us
    dot_general x16, matrix products, key_step(): jnp.einsum('rgmc,kgc->gmrk', query_row_block, key_blk, preferred_element_...  21.3 us
  transfers between devices with their start and end apart: 51, of which 49 were waited for; matrix products, arithmetic and copies ran while one was open for 9% of the time, Pallas kernels for 0%

commit v1 on v0

v1 whole, which is shorter than its diff:
```python
import functools

import jax
import jax.numpy as jnp
from jax import lax
from jax.experimental import pallas as pl
from jax.experimental.pallas import tpu as pltpu
from jax.sharding import PartitionSpec as P

QUERY_HEADS = 40
KEY_VALUE_HEADS = 8
HEAD_SIZE = 128
BALANCED_TOKENS = 128
GROUP = QUERY_HEADS // KEY_VALUE_HEADS
LOG2E = 1.4426950408889634
ROWS = 128
BAND = 16
OWNERS = 16


def attention_kernel(
    meta_ref, qd_ref, lse_ref, delta_ref, kv_ref, dq_ref, dkv_ref, q_sc, g_sc, dq_sc, acc
):
    first = meta_ref[0]
    count = meta_ref[1]
    owners = kv_ref.shape[0]
    blocks = q_sc.shape[0]
    stacked = GROUP * ROWS
    chunk = OWNERS * BAND
    scale = HEAD_SIZE ** (-0.5)
    row_span = BAND * owners
    acc[...] = jnp.zeros_like(acc)
    dq_sc[...] = jnp.zeros_like(dq_sc)
    for b in range(blocks):
        live = (lax.broadcasted_iota(jnp.int32, (ROWS, HEAD_SIZE), 0) + b * ROWS) < count
        for m in range(GROUP):
            rows = pl.ds(b * ROWS, ROWS)
            q = qd_ref[rows, pl.ds(m * HEAD_SIZE, HEAD_SIZE)]
            g = qd_ref[rows, pl.ds((GROUP + m) * HEAD_SIZE, HEAD_SIZE)]
            zero = jnp.zeros((), jnp.float32)
            q_sc[b, pl.ds(m * ROWS, ROWS), :] = jnp.where(
                live, q.astype(jnp.float32), zero
            ).astype(jnp.bfloat16)
            g_sc[b, pl.ds(m * ROWS, ROWS), :] = jnp.where(
                live, g.astype(jnp.float32), zero
            ).astype(jnp.bfloat16)
    live_blocks = (count + ROWS - 1) // ROWS
    key_blocks = (first + count + row_span - 1) // row_span
    index = lax.broadcasted_iota(jnp.int32, (chunk, stacked), 0)
    key_local = (index % BAND) * owners + index // BAND
    row_local = lax.broadcasted_iota(jnp.int32, (chunk, stacked), 1) % ROWS
    gap = key_local - row_local

    def key_block(j, carry):
        lowest = jnp.maximum(j * row_span - first, 0) // ROWS
        band = pl.ds(pl.multiple_of(j * BAND, BAND), BAND)
        for c in range(owners // OWNERS):
            own = pl.ds(c * OWNERS, OWNERS)
            key = kv_ref[own, band, pl.ds(0, HEAD_SIZE)].reshape(chunk, HEAD_SIZE)
            value = kv_ref[own, band, pl.ds(HEAD_SIZE, HEAD_SIZE)].reshape(chunk, HEAD_SIZE)
            key_t = key.astype(jnp.float32).T.astype(jnp.bfloat16)

            def row_block(b, inner):
                q = q_sc[b]
                g = g_sc[b]
                nt = (((1,), (1,)), ((), ()))
                nn = (((1,), (0,)), ((), ()))
                f32 = jnp.float32
                score = lax.dot_general(key, q, nt, preferred_element_type=f32)
                dprob = lax.dot_general(value, g, nt, preferred_element_type=f32)
                limit = first + b * ROWS - j * row_span - c * OWNERS
                prob = jnp.where(
                    gap <= limit,
                    jnp.exp2(score * (scale * LOG2E) - lse_ref[pl.ds(b, 1), :]),
                    0.0,
                )
                dscore = prob * (dprob - delta_ref[pl.ds(b, 1), :])
                prob_low = prob.astype(jnp.bfloat16)
                dscore_low = dscore.astype(jnp.bfloat16)
                dk = lax.dot_general(dscore_low, q, nn, preferred_element_type=f32)
                dv = lax.dot_general(prob_low, g, nn, preferred_element_type=f32)
                acc[own, band, pl.ds(0, HEAD_SIZE)] += dk.reshape(OWNERS, BAND, HEAD_SIZE)
                acc[own, band, pl.ds(HEAD_SIZE, HEAD_SIZE)] += dv.reshape(OWNERS, BAND, HEAD_SIZE)
                dq_sc[b] += lax.dot_general(key_t, dscore_low, nn, preferred_element_type=f32)
                return inner

            lax.fori_loop(lowest, live_blocks, row_block, 0)
        return carry

    lax.fori_loop(0, key_blocks, key_block, 0)
    for b in range(blocks):
        for m in range(GROUP):
            part = dq_sc[b, :, pl.ds(m * ROWS, ROWS)].T * scale
            dq_ref[pl.ds(b * ROWS, ROWS), pl.ds(m * HEAD_SIZE, HEAD_SIZE)] = part.astype(
                dq_ref.dtype
            )
    dkv_ref[:, :, pl.ds(0, HEAD_SIZE)] = (acc[:, :, pl.ds(0, HEAD_SIZE)] * scale).astype(
        dkv_ref.dtype
    )
    dkv_ref[:, :, pl.ds(HEAD_SIZE, HEAD_SIZE)] = acc[:, :, pl.ds(HEAD_SIZE, HEAD_SIZE)].astype(
        dkv_ref.dtype
    )


def attention(meta, qd, lse, delta, kv, interpret=False):
    capacity = qd.shape[0]
    owners, per_owner, width = kv.shape
    blocks = capacity // ROWS
    vmem = pl.BlockSpec(memory_space=pltpu.VMEM)
    return pl.pallas_call(
        attention_kernel,
        name="attention",
        out_shape=(
            jax.ShapeDtypeStruct((capacity, GROUP * HEAD_SIZE), jnp.bfloat16),
            jax.ShapeDtypeStruct(kv.shape, jnp.bfloat16),
        ),
        in_specs=[pl.BlockSpec(memory_space=pltpu.SMEM), vmem, vmem, vmem, vmem],
        out_specs=(vmem, vmem),
        scratch_shapes=[
            pltpu.VMEM((blocks, GROUP * ROWS, HEAD_SIZE), jnp.bfloat16),
            pltpu.VMEM((blocks, GROUP * ROWS, HEAD_SIZE), jnp.bfloat16),
            pltpu.VMEM((blocks, HEAD_SIZE, GROUP * ROWS), jnp.float32),
            pltpu.VMEM(kv.shape, jnp.float32),
        ],
        compiler_params=pltpu.CompilerParams(vmem_limit_bytes=56 << 20),
        cost_estimate=pl.CostEstimate(
            flops=10 * capacity * GROUP * HEAD_SIZE * owners * per_owner // 2,
            bytes_accessed=2 * (2 * kv.size + 3 * qd.size),
            transcendentals=0,
        ),
        interpret=interpret,
    )(meta, qd, lse, delta, kv)


def per_device(queries, keys, values, outputs, output_gradient, lse, ranks):
    owners = lax.axis_size("seq")
    heads = lax.axis_size("head")
    me = lax.axis_index("seq")
    home_rows = queries.shape[0]
    capacity = home_rows * heads
    slots = capacity // owners
    survivors = BALANCED_TOKENS * owners
    bf16 = jnp.bfloat16
    width = 2 * HEAD_SIZE
    exchange = functools.partial(lax.all_to_all, split_axis=0, concat_axis=0, tiled=True)

    dots = jnp.sum(
        output_gradient.astype(jnp.float32).reshape(home_rows, QUERY_HEADS, HEAD_SIZE)
        * outputs.astype(jnp.float32).reshape(home_rows, QUERY_HEADS, HEAD_SIZE),
        axis=-1,
    ).astype(bf16)

    def by_head(array):
        return array.reshape(home_rows, heads, -1).transpose(1, 0, 2)

    living = jnp.sum((ranks < survivors).astype(jnp.int32))
    digits = jnp.stack([ranks[0] // 128, ranks[0] % 128, living]).astype(bf16)
    small = jnp.concatenate([by_head(lse), by_head(dots)], axis=-1).transpose(0, 2, 1)
    small = jnp.pad(small, ((0, 0), (0, 0), (0, width - home_rows)))
    digit_rows = jnp.broadcast_to(
        jnp.pad(digits, (0, width - 3))[None, None], (heads, 16 - 2 * GROUP, width)
    )
    first_pack = jnp.concatenate(
        [jnp.concatenate([by_head(keys), by_head(values)], axis=-1), small, digit_rows], axis=1
    )
    first_pack = exchange(first_pack, "head")
    pairs = first_pack[:, :home_rows].reshape(slots, owners, width)
    extra = first_pack[:, home_rows:].astype(jnp.float32)
    first_rank = (extra[0, 2 * GROUP, 0] * 128 + extra[0, 2 * GROUP, 1]).astype(jnp.int32)
    count = jnp.sum(extra[:, 2 * GROUP, 2]).astype(jnp.int32)

    turn = first_rank % owners
    by_owner = pairs.transpose(1, 0, 2)
    by_owner = lax.dynamic_slice_in_dim(
        jnp.concatenate([by_owner, by_owner], axis=0), owners - turn, owners, 0
    )
    head_digits = jnp.stack(
        [first_rank // 128, first_rank % 128, count // 128, count % 128]
    ).astype(bf16)
    tail = jnp.broadcast_to(
        jnp.pad(head_digits, (0, width - 4))[None, None], (owners, 8 - slots, width)
    )
    arrived = exchange(jnp.concatenate([by_owner, tail], axis=1), "seq")
    told = arrived[:, slots].astype(jnp.float32)
    starts = (told[:, 0] * 128 + told[:, 1]).astype(jnp.int32)
    counts = (told[:, 2] * 128 + told[:, 3]).astype(jnp.int32)
    within = jnp.arange(8, dtype=jnp.int32)[None, :] * owners + ((me - starts) % owners)[:, None]
    alive = (within < counts[:, None]) & (jnp.arange(8) < slots)[None, :]
    target = jnp.where(alive, (starts[:, None] + within) // owners, -1).reshape(-1)
    pick = (target[None, :] == jnp.arange(BALANCED_TOKENS, dtype=jnp.int32)[:, None]).astype(bf16)
    placed = jnp.dot(
        pick, arrived.reshape(owners * 8, width), preferred_element_type=jnp.float32
    ).astype(bf16)
    all_kv = lax.all_gather(placed, "seq", axis=0, tiled=False)

    placed_first, queries, output_gradient = lax.optimization_barrier(
        (placed, queries, output_gradient)
    )
    qd = exchange(
        jnp.concatenate([by_head(queries), by_head(output_gradient)], axis=-1), "head"
    ).reshape(capacity, 2 * GROUP * HEAD_SIZE)

    slot = jnp.arange(capacity, dtype=jnp.int32)
    per_row = extra[:, : 2 * GROUP, :home_rows].transpose(1, 0, 2).reshape(2 * GROUP, capacity)
    per_row = jnp.where(slot[None, :] < count, per_row, 0.0)
    per_row = per_row.reshape(2, GROUP, capacity // ROWS, ROWS).transpose(0, 2, 1, 3)
    per_row = per_row.reshape(2, capacity // ROWS, GROUP * ROWS)
    dq, dkv = attention(
        jnp.stack([first_rank, count]), qd, per_row[0] * LOG2E, per_row[1], all_kv
    )

    parts = exchange(dkv, "seq")
    summed = jnp.sum(parts.astype(jnp.float32), axis=0).astype(bf16)
    back = lax.dot_general(
        pick, summed, (((0,), (0,)), ((), ())), preferred_element_type=jnp.float32
    ).astype(bf16)
    back = exchange(back.reshape(owners, 8, width), "seq")
    back = lax.dynamic_slice_in_dim(jnp.concatenate([back, back], axis=0), turn, owners, 0)
    back = back[:, :slots].transpose(1, 0, 2).reshape(heads, home_rows, width)
    back = exchange(back, "head")
    dq = exchange(dq.reshape(heads, home_rows, GROUP * HEAD_SIZE), "head")
    query_grads = dq.transpose(1, 0, 2).reshape(home_rows, -1)
    key_grads = back[:, :, :HEAD_SIZE].transpose(1, 0, 2).reshape(home_rows, -1)
    value_grads = back[:, :, HEAD_SIZE:].transpose(1, 0, 2).reshape(home_rows, -1)
    return (query_grads, key_grads, value_grads)


def solution(mesh):
    placed = P(("seq", "head"), None)
    return jax.shard_map(
        per_device,
        mesh=mesh,
        in_specs=(placed,) * 6 + (P(("seq", "head")),),
        out_specs=(placed,) * 3,
        check_vma=False,
    )
```

time: 1040 us -> 377 us (0.36)
  waiting for transfers between devices: 563 us -> 108 us
  starting transfers between devices: 233 us -> 30.1 us
  blocking collectives: 53.3 us -> 191 us
  matrix products: 95 us -> 1.1 us
  local copies, waits for them, and re-layouts: 49.2 us -> 6.97 us
  loops' own time: 11.9 us -> 0 us
    all_to_all x49 -> x4, waiting for transfers between devices: 563 us -> 64.5 us  [the longest x1 26.3 us: per_device(): exchange(jnp.concatenate([by_head(queries), by_head(output_gradient)], ax...]
    all_to_all x49 -> x4, starting transfers between devices: 233 us -> 30 us  [the longest x1 16.6 us: per_device(): arrived = exchange(jnp.concatenate([by_owner, tail], axis=1), 'seq')]
    all_to_all x1 -> x3, blocking collectives: 15.7 us -> 191 us  [the longest x1 154 us: per_device(): parts = exchange(dkv, 'seq')]
    dot_general x80 -> x2, matrix products: 95 us -> 1.1 us  [the longest x1 0.83 us: per_device(): jnp.dot(pick, arrived.reshape(owners * 8, width), preferred_element_type=...]
    all_gather x2 -> x1, waiting for transfers between devices: 0.04 us -> 43.4 us  [per_device(): all_kv = lax.all_gather(placed, 'seq', axis=0, tiled=False)]
    unnamed x2 -> x0, blocking collectives: 37.6 us -> none
    dynamic_slice x22 -> x0, local copies, waits for them, and re-layouts: 15 us -> none  [the longest x16 9.32 us: per_device(): lax.scan(outer_step, start_acc, jnp.arange(outer, dtype=jnp.int32))]
    scatter x8 -> x0, local copies, waits for them, and re-layouts: 12.4 us -> none  [place(): return jnp.zeros((BALANCED_TOKENS, width), array.dtype).at[target_rank].s...]
  transfers between devices with their start and end apart: 51 -> 5, of which waited for: 49 -> 5; matrix products, arithmetic and copies ran while one was open for 9% -> 1% of each run, Pallas kernels for 0% -> 0%
where the time goes in v1:
time: 377 us; the launch traced here: 376 us
  blocking collectives  191 us (51%)
  waiting for transfers between devices  108 us (29%)
  starting transfers between devices  30.1 us (8%)
  between operations  19.6 us (5%)
  other arithmetic  10.3 us (3%)
  Pallas kernels  9.56 us (3%)
  local copies, waits for them, and re-layouts  6.97 us (2%)
    all_to_all x1, blocking collectives, per_device(): parts = exchange(dkv, 'seq')  154 us
    all_gather x1, waiting for transfers between devices, per_device(): all_kv = lax.all_gather(placed, 'seq', axis=0, tiled=False)  43.4 us
    all_to_all x1, waiting for transfers between devices, per_device(): exchange(jnp.concatenate([by_head(queries), by_head(output_gradient)], ax...  26.3 us
    all_to_all x1, blocking collectives, per_device(): back = exchange(back.reshape(owners, 8, width), 'seq')  19.8 us
    all_to_all x1, blocking collectives, per_device(): first_pack = exchange(first_pack, 'head')  17 us
    all_to_all x1, starting transfers between devices, per_device(): arrived = exchange(jnp.concatenate([by_owner, tail], axis=1), 'seq')  16.6 us
    all_to_all x1, waiting for transfers between devices, per_device(): dq = exchange(dq.reshape(heads, home_rows, GROUP * HEAD_SIZE), 'head')  16.4 us
    all_to_all x1, waiting for transfers between devices, per_device(): arrived = exchange(jnp.concatenate([by_owner, tail], axis=1), 'seq')  13 us
  transfers between devices with their start and end apart: 5, of which 5 were waited for; matrix products, arithmetic and copies ran while one was open for 1% of the time, Pallas kernels for 0%

profile of v1, /device:TPU:1, one launch (start us, length us, event | category | flops | bytes accessed | tf_op | source)
XLA Modules:
  0.0 376.5 jit_solution(14726118021082147564)
XLA Ops:
  7.2 1.3 fusion.33
  11.7 0.7 reshape.150
  12.4 0.9 copy.62
  13.4 0.9 copy.63
  14.3 1.3 multiply_bitcast_fusion
  15.8 0.3 reduce_sum.39
  16.4 17.0 %all_to_all.35 = bf16[8,64,256]{2,1,0:T(8,128)(2,1)S(1)} all-to-all(bf16[8,64,256]{2,1,0:T(8,128)(2,1)S(1)} %copy.46), channel_id=1, replica_groups=mesh['seq'=64,'head'=8] {'head'}, dimensions={0} | all-to-all | bytes 524288 | tf_op jit(solution)/shard_map/all_to_all | solution.py:166
  33.4 0.7 slice_reduce_fusion
  34.8 0.6 fusion.34
  37.1 0.9 copy.47
  37.9 16.6 %all-to-all-start.1 = ((bf16[64,8,256]{2,1,0:T(8,128)(2,1)}), bf16[64,8,256]{2,1,0:T(8,128)(2,1)S(1)}, u32[]{:S(2)}, u32[]{:S(2)}) async-start(bf16[64,8,256]{2,1,0:T(8,128)(2,1)} %copy.47), calls=%async_computation.1 | async-start | bytes 524288 | tf_op jit(solution)/shard_map/all_to_all | solution.py:183
  54.6 13.0 %all-to-all-done.1 = bf16[64,8,256]{2,1,0:T(8,128)(2,1)S(1)} async-done(((bf16[64,8,256]{2,1,0:T(8,128)(2,1)}), bf16[64,8,256]{2,1,0:T(8,128)(2,1)S(1)}, u32[]{:S(2)}, u32[]{:S(2)}) %all-to-all-start.1) | async-done | bytes 262176 | tf_op jit(solution)/shard_map/all_to_all | solution.py:183
  68.3 0.8 convolution_convert_fusion.1
  69.3 1.0 pad_maximum_fusion
  70.3 3.6 all-to-all-start.2
  74.0 0.6 pad_add_fusion.meta_ref
  74.7 0.6 slice_bitcast_fusion.3
  75.3 26.3 %all-to-all-done.2 = bf16[8,48,1280]{2,1,0:T(8,128)(2,1)S(1)} async-done(((bf16[8,48,1280]{2,1,0:T(8,128)(2,1)}), bf16[8,48,1280]{2,1,0:T(8,128)(2,1)S(1)}, u32[]{:S(2)}, u32[]{:S(2)}) %all-to-all-start.2) | async-done | bytes 983072 | tf_op jit(solution)/shard_map/all_to_all | solution.py:199
  101.6 43.4 %all-gather.3.cloned.1.call-done = bf16[8192,256]{1,0:T(8,128)(2,1)} async-done(((bf16[128,256]{1,0:T(8,128)(2,1)}), bf16[8192,256]{1,0:T(8,128)(2,1)}) %all-gather.3.cloned.1.call-update) | async-done | bytes 4194320 | tf_op jit(solution)/shard_map/all_gather | solution.py:194
  145.0 9.6 %attention.1 = (bf16[384,640]{1,0:T(8,128)(2,1)}, bf16[64,128,256]{2,1,0:T(8,128)(2,1)}) custom-call(s32[2]{0:T(128)} %pad_add_fusion.meta_ref, bf16[384,1280]{1,0:T(8,128)(2,1)} %bitcast.93, f32[3,640]{1,0:T(4,128)} %get-tuple-element.19.lse_ref, f32[3,640]{1,0:T(4,128)} %get-tuple-element.18.delta_ref, bf16[64,128,256]{2,1,0:T(8,128)(2,1)} %bitcast.108), custom_call_target="tpu_custom_call" | custom-call | flops 10066329600 | bytes 11337728 | tf_op jit(solution)/shard_map/attention/pallas_call | solution.py:110
  154.6 154.1 %all_to_all.36 = bf16[64,128,256]{2,1,0:T(8,128)(2,1)} all-to-all(bf16[64,128,256]{2,1,0:T(8,128)(2,1)} %get-tuple-element.10), channel_id=1, replica_groups=mesh['seq'=64,'head'=8] {'seq'}, dimensions={0} | all-to-all | bytes 8388608 | tf_op jit(solution)/shard_map/all_to_all | solution.py:212
  308.7 2.8 reduce_sum.42
  311.5 0.3 fusion
  311.8 19.8 %all_to_all.37 = bf16[64,8,256]{2,1,0:T(8,128)(2,1)S(1)} all-to-all(bf16[64,8,256]{2,1,0:T(8,128)(2,1)S(1)} %fusion), channel_id=1, replica_groups=mesh['seq'=64,'head'=8] {'seq'}, dimensions={0} | all-to-all | bytes 524288 | tf_op jit(solution)/shard_map/all_to_all | solution.py:217
  331.6 6.5 %all-to-all-start.3 = ((bf16[8,48,640]{2,1,0:T(8,128)(2,1)}), bf16[8,48,640]{2,1,0:T(8,128)(2,1)S(1)}, u32[]{:S(2)}, u32[]{:S(2)}) async-start(bf16[8,48,640]{2,1,0:T(8,128)(2,1)} %bitcast.27), calls=%async_computation.3 | async-start | bytes 983040 | tf_op jit(solution)/shard_map/all_to_all | solution.py:221
  338.1 0.8 fusion.7
  338.9 16.4 %all-to-all-done.3 = bf16[8,48,640]{2,1,0:T(8,128)(2,1)S(1)} async-done(((bf16[8,48,640]{2,1,0:T(8,128)(2,1)}), bf16[8,48,640]{2,1,0:T(8,128)(2,1)S(1)}, u32[]{:S(2)}, u32[]{:S(2)}) %all-to-all-start.3) | async-done | bytes 491552 | tf_op jit(solution)/shard_map/all_to_all | solution.py:221
  355.3 3.4 all-to-all-start.6
  358.7 0.8 copy.59
  359.5 8.7 %all-to-all-done.6 = bf16[8,48,256]{2,1,0:T(8,128)(2,1)S(1)} async-done(((bf16[8,48,256]{2,1,0:T(8,128)(2,1)}), bf16[8,48,256]{2,1,0:T(8,128)(2,1)S(1)}, u32[]{:S(2)}, u32[]{:S(2)}) %all-to-all-start.6) | async-done | bytes 196640 | tf_op jit(solution)/shard_map/all_to_all | solution.py:220
  368.3 0.7 copy.74
  369.0 0.7 copy.75
  (42 shorter events, 1.8 us)
Async XLA Ops:
  15.6 53.6 %copy-start = (bf16[48,5120]{1,0:T(8,128)(2,1)S(1)}, bf16[48,5120]{1,0:T(8,128)(2,1)}, u32[]{:S(2)}) copy-start(bf16[48,5120]{1,0:T(8,128)(2,1)} %param.11) | copy-start | bytes 1474564
  15.6 53.7 %copy-start.2 = (bf16[48,5120]{1,0:T(8,128)(2,1)S(1)}, bf16[48,5120]{1,0:T(8,128)(2,1)}, u32[]{:S(2)}) copy-start(bf16[48,5120]{1,0:T(8,128)(2,1)} %param.7) | copy-start | bytes 1474564
  37.9 29.7 %all-to-all-start.1 = ((bf16[64,8,256]{2,1,0:T(8,128)(2,1)}), bf16[64,8,256]{2,1,0:T(8,128)(2,1)S(1)}, u32[]{:S(2)}, u32[]{:S(2)}) async-start(bf16[64,8,256]{2,1,0:T(8,128)(2,1)} %copy.47), calls=%async_computation.1 | async-start | bytes 524288 | tf_op jit(solution)/shard_map/all_to_all | solution.py:183
  54.5 90.5 %all-gather.3.cloned.1.call-start = ((), (), s32[]{:S(2)}) async-start(), calls=%async_computation.7 | async-start | bytes 4259840 | tf_op jit(solution)/shard_map/all_gather | solution.py:194
  70.3 31.3 %all-to-all-start.2 = ((bf16[8,48,1280]{2,1,0:T(8,128)(2,1)}), bf16[8,48,1280]{2,1,0:T(8,128)(2,1)S(1)}, u32[]{:S(2)}, u32[]{:S(2)}) async-start(bf16[8,48,1280]{2,1,0:T(8,128)(2,1)} %pad_maximum_fusion), calls=%async_computation.2 | async-start | bytes 1966080 | tf_op jit(solution)/shard_map/all_to_all | solution.py:199
  101.6 43.4 %copy-start.1 = (bf16[8,48,1280]{2,1,0:T(8,128)(2,1)}, bf16[8,48,1280]{2,1,0:T(8,128)(2,1)S(1)}, u32[]{:S(2)}) copy-start(bf16[8,48,1280]{2,1,0:T(8,128)(2,1)S(1)} %all-to-all-done.2) | copy-start | bytes 2949124
  331.6 23.7 %all-to-all-start.3 = ((bf16[8,48,640]{2,1,0:T(8,128)(2,1)}), bf16[8,48,640]{2,1,0:T(8,128)(2,1)S(1)}, u32[]{:S(2)}, u32[]{:S(2)}) async-start(bf16[8,48,640]{2,1,0:T(8,128)(2,1)} %bitcast.27), calls=%async_computation.3 | async-start | bytes 983040 | tf_op jit(solution)/shard_map/all_to_all | solution.py:221
  355.3 13.0 %all-to-all-start.6 = ((bf16[8,48,256]{2,1,0:T(8,128)(2,1)}), bf16[8,48,256]{2,1,0:T(8,128)(2,1)S(1)}, u32[]{:S(2)}, u32[]{:S(2)}) async-start(bf16[8,48,256]{2,1,0:T(8,128)(2,1)} %bitcast.31), calls=%async_computation.6 | async-start | bytes 393216 | tf_op jit(solution)/shard_map/all_to_all | solution.py:220
Sparse Core Ops, SparseCore 0:
  69.3 75.6 all-gather.2

commit v2 on v1

--- a/solution.py
+++ b/solution.py
@@ -47,7 +47,8 @@
     live_blocks = (count + ROWS - 1) // ROWS
     key_blocks = (first + count + row_span - 1) // row_span
     index = lax.broadcasted_iota(jnp.int32, (chunk, stacked), 0)
-    key_local = (index % BAND) * owners + index // BAND
+    place_in = index // BAND
+    key_local = (index % BAND) * owners + (place_in // 4) * 8 + (place_in % 4) * 2
     row_local = lax.broadcasted_iota(jnp.int32, (chunk, stacked), 1) % ROWS
     gap = key_local - row_local
 
@@ -68,7 +69,7 @@
                 f32 = jnp.float32
                 score = lax.dot_general(key, q, nt, preferred_element_type=f32)
                 dprob = lax.dot_general(value, g, nt, preferred_element_type=f32)
-                limit = first + b * ROWS - j * row_span - c * OWNERS
+                limit = first + b * ROWS - j * row_span - (c % 2) * 32 - c // 2
                 prob = jnp.where(
                     gap <= limit,
                     jnp.exp2(score * (scale * LOG2E) - lse_ref[pl.ds(b, 1), :]),
@@ -132,6 +133,223 @@
     )(meta, qd, lse, delta, kv)
 
 
+def place(seq_index):
+    return seq_index // 8, (seq_index // 2) % 4, seq_index % 2
+
+
+def peers():
+    seq = lax.axis_index("seq")
+    head = lax.axis_index("head")
+    z, x, core = place(seq)
+    spot = lambda z, x, core: (z * 8 + x * 2 + core, head)
+    to_z = [None] + [spot((z + d) % 8, x, core) for d in range(1, 8)]
+    to_x = [None] + [spot(z, (x + e) % 4, core) for e in range(1, 4)]
+    partner = spot(z, x, 1 - core)
+    to_head = [None] + [(seq, (head + d) % 8) for d in range(1, 8)]
+    return z, x, core, head, to_z, to_x, partner, to_head
+
+
+def meet(groups):
+    barrier = pltpu.get_barrier_semaphore()
+    total = 0
+    for group in groups:
+        for device in group:
+            pl.semaphore_signal(
+                barrier, inc=1, device_id=device, device_id_type=pl.DeviceIdType.MESH
+            )
+            total += 1
+    pl.semaphore_wait(barrier, total)
+
+
+def remote(src, dst, send, recv, device):
+    return pltpu.make_async_remote_copy(
+        src_ref=src,
+        dst_ref=dst,
+        send_sem=send,
+        recv_sem=recv,
+        device_id=device,
+        device_id_type=pl.DeviceIdType.MESH,
+    )
+
+
+NEAR_FIRST = (0, 1, 7, 2, 6, 3, 5, 4)
+
+
+def gather_kernel(
+    own_ref, qd_ref, kv_ref, rows_ref, own_sem, z_send, z_recv, x_send, x_recv, p_send, p_recv,
+    h_send, h_recv,
+):
+    z, x, core, head, to_z, to_x, partner, to_head = peers()
+    meet((to_z[1:], to_x[1:], (partner,), to_head[1:]))
+    copies = []
+    for d in NEAR_FIRST[1:]:
+        copy = remote(own_ref, kv_ref.at[core, z, x], z_send.at[d], z_recv.at[d], to_z[d])
+        copy.start()
+        copies.append(copy)
+    for d in NEAR_FIRST[1:]:
+        copy = remote(
+            qd_ref.at[(head + d) % 8], rows_ref.at[head], h_send.at[d], h_recv.at[d], to_head[d]
+        )
+        copy.start()
+        copies.append(copy)
+    mine = pltpu.make_async_copy(own_ref, kv_ref.at[core, z, x], own_sem.at[0])
+    mine.start()
+    kept = pltpu.make_async_copy(qd_ref.at[head], rows_ref.at[head], own_sem.at[1])
+    kept.start()
+    for d in NEAR_FIRST:
+        source = (z + 8 - d) % 8
+        block = kv_ref.at[core, source, x]
+        if d == 0:
+            mine.wait()
+        else:
+            remote(own_ref, block, z_send.at[d], z_recv.at[d], to_z[d]).wait_recv()
+        for e in (1, 3, 2):
+            copy = remote(block, block, x_send.at[d, e], x_recv.at[d, e], to_x[e])
+            copy.start()
+            copies.append(copy)
+    for d in NEAR_FIRST:
+        source = (z + 8 - d) % 8
+        for e in (1, 3, 2):
+            block = kv_ref.at[core, source, (x + 4 - e) % 4]
+            remote(block, block, x_send.at[d, e], x_recv.at[d, e], to_x[e]).wait_recv()
+        row = kv_ref.at[core, source]
+        copy = remote(row, row, p_send.at[d], p_recv.at[d], partner)
+        copy.start()
+        copies.append(copy)
+    for d in NEAR_FIRST:
+        row = kv_ref.at[1 - core, (z + 8 - d) % 8]
+        remote(row, row, p_send.at[d], p_recv.at[d], partner).wait_recv()
+    for d in NEAR_FIRST[1:]:
+        part = rows_ref.at[(head + 8 - d) % 8]
+        remote(part, part, h_send.at[d], h_recv.at[d], to_head[d]).wait_recv()
+    kept.wait()
+    for copy in copies:
+        copy.wait_send()
+
+
+def gather(own, qd):
+    vmem = pl.BlockSpec(memory_space=pltpu.VMEM)
+    dma = pltpu.SemaphoreType.DMA
+    return pl.pallas_call(
+        gather_kernel,
+        name="gather",
+        out_shape=(
+            jax.ShapeDtypeStruct((2, 8, 4) + own.shape, own.dtype),
+            jax.ShapeDtypeStruct(qd.shape, qd.dtype),
+        ),
+        in_specs=[vmem, vmem],
+        out_specs=(vmem, vmem),
+        scratch_shapes=[
+            dma((2,)), dma((8,)), dma((8,)), dma((8, 4)), dma((8, 4)), dma((8,)), dma((8,)),
+            dma((8,)), dma((8,)),
+        ],
+        compiler_params=pltpu.CompilerParams(
+            collective_id=0, has_side_effects=True, vmem_limit_bytes=32 << 20
+        ),
+    )(own, qd)
+
+
+def reduce_kernel(
+    kv_ref, dq_ref, sum_ref, rows_ref, from_core, to_row, from_row, to_column, from_column, total,
+    own_sem, p_send, p_recv, x_send, x_recv, z_send, z_recv, h_send, h_recv,
+):
+    z, x, core, head, to_z, to_x, partner, to_head = peers()
+    f32 = jnp.float32
+    meet((to_z[1:], to_x[1:], (partner,), to_head[1:]))
+    order = (4, 3, 5, 2, 6, 1, 7, 0)
+    copies = []
+    for d in order:
+        there = (z + d) % 8
+        copy = remote(
+            kv_ref.at[1 - core, there], from_core.at[there], p_send.at[d], p_recv.at[d], partner
+        )
+        copy.start()
+        copies.append(copy)
+    for d in NEAR_FIRST[1:]:
+        copy = remote(
+            dq_ref.at[(head + d) % 8], rows_ref.at[head], h_send.at[d], h_recv.at[d], to_head[d]
+        )
+        copy.start()
+        copies.append(copy)
+    kept = pltpu.make_async_copy(dq_ref.at[head], rows_ref.at[head], own_sem.at[0])
+    kept.start()
+    for d in order:
+        there = (z + d) % 8
+        remote(
+            kv_ref.at[1 - core, there], from_core.at[there], p_send.at[d], p_recv.at[d], partner
+        ).wait_recv()
+        for e in (2, 1, 3):
+            other = (x + e) % 4
+            to_row[e, d] = (
+                kv_ref[core, there, other].astype(f32) + from_core[there, other].astype(f32)
+            ).astype(to_row.dtype)
+            copy = remote(
+                to_row.at[e, d], from_row.at[e, d], x_send.at[e, d], x_recv.at[e, d], to_x[e]
+            )
+            copy.start()
+            copies.append(copy)
+    for d in order:
+        there = (z + d) % 8
+        part = kv_ref[core, there, x].astype(f32) + from_core[there, x].astype(f32)
+        for e in (1, 3, 2):
+            remote(
+                to_row.at[e, d], from_row.at[e, d], x_send.at[e, d], x_recv.at[e, d], to_x[e]
+            ).wait_recv()
+            part = part + from_row[e, d].astype(f32)
+        if d == 0:
+            total[...] = part
+        else:
+            to_column[d] = part.astype(to_column.dtype)
+            copy = remote(
+                to_column.at[d], from_column.at[d], z_send.at[d], z_recv.at[d], to_z[d]
+            )
+            copy.start()
+            copies.append(copy)
+    part = total[...]
+    for d in order[:-1]:
+        remote(
+            to_column.at[d], from_column.at[d], z_send.at[d], z_recv.at[d], to_z[d]
+        ).wait_recv()
+        part = part + from_column[d].astype(f32)
+    sum_ref[...] = part.astype(sum_ref.dtype)
+    for d in NEAR_FIRST[1:]:
+        piece = rows_ref.at[(head + 8 - d) % 8]
+        remote(piece, piece, h_send.at[d], h_recv.at[d], to_head[d]).wait_recv()
+    kept.wait()
+    for copy in copies:
+        copy.wait_send()
+
+
+def reduce(dkv, dq):
+    vmem = pl.BlockSpec(memory_space=pltpu.VMEM)
+    dma = pltpu.SemaphoreType.DMA
+    block = dkv.shape[3:]
+    bf16 = jnp.bfloat16
+    return pl.pallas_call(
+        reduce_kernel,
+        name="reduce",
+        out_shape=(
+            jax.ShapeDtypeStruct(block, bf16),
+            jax.ShapeDtypeStruct(dq.shape, dq.dtype),
+        ),
+        in_specs=[vmem, vmem],
+        out_specs=(vmem, vmem),
+        scratch_shapes=[
+            pltpu.VMEM((8, 4) + block, bf16),
+            pltpu.VMEM((4, 8) + block, bf16),
+            pltpu.VMEM((4, 8) + block, bf16),
+            pltpu.VMEM((8,) + block, bf16),
+            pltpu.VMEM((8,) + block, bf16),
+            pltpu.VMEM(block, jnp.float32),
+            dma((1,)), dma((8,)), dma((8,)), dma((4, 8)), dma((4, 8)), dma((8,)), dma((8,)),
+            dma((8,)), dma((8,)),
+        ],
+        compiler_params=pltpu.CompilerParams(
+            collective_id=1, has_side_effects=True, vmem_limit_bytes=40 << 20
+        ),
+    )(dkv, dq)
+
+
 def per_device(queries, keys, values, outputs, output_gradient, lse, ranks):
     owners = lax.axis_size("seq")
     heads = lax.axis_size("head")
@@ -191,14 +409,11 @@
     placed = jnp.dot(
         pick, arrived.reshape(owners * 8, width), preferred_element_type=jnp.float32
     ).astype(bf16)
-    all_kv = lax.all_gather(placed, "seq", axis=0, tiled=False)
-
-    placed_first, queries, output_gradient = lax.optimization_barrier(
-        (placed, queries, output_gradient)
-    )
-    qd = exchange(
-        jnp.concatenate([by_head(queries), by_head(output_gradient)], axis=-1), "head"
-    ).reshape(capacity, 2 * GROUP * HEAD_SIZE)
+    all_kv, qd = gather(
+        placed, jnp.concatenate([by_head(queries), by_head(output_gradient)], axis=-1)
+    )
+    all_kv = all_kv.reshape(owners, BALANCED_TOKENS, width)
+    qd = qd.reshape(capacity, 2 * GROUP * HEAD_SIZE)
 
     slot = jnp.arange(capacity, dtype=jnp.int32)
     per_row = extra[:, : 2 * GROUP, :home_rows].transpose(1, 0, 2).reshape(2 * GROUP, capacity)
@@ -209,8 +424,10 @@
         jnp.stack([first_rank, count]), qd, per_row[0] * LOG2E, per_row[1], all_kv
     )
 
-    parts = exchange(dkv, "seq")
-    summed = jnp.sum(parts.astype(jnp.float32), axis=0).astype(bf16)
+    summed, dq = reduce(
+        dkv.reshape(2, 8, 4, BALANCED_TOKENS, width),
+        dq.reshape(heads, home_rows, GROUP * HEAD_SIZE),
+    )
     back = lax.dot_general(
         pick, summed, (((0,), (0,)), ((), ())), preferred_element_type=jnp.float32
     ).astype(bf16)
@@ -218,7 +435,6 @@
     back = lax.dynamic_slice_in_dim(jnp.concatenate([back, back], axis=0), turn, owners, 0)
     back = back[:, :slots].transpose(1, 0, 2).reshape(heads, home_rows, width)
     back = exchange(back, "head")
-    dq = exchange(dq.reshape(heads, home_rows, GROUP * HEAD_SIZE), "head")
     query_grads = dq.transpose(1, 0, 2).reshape(home_rows, -1)
     key_grads = back[:, :, :HEAD_SIZE].transpose(1, 0, 2).reshape(home_rows, -1)
     value_grads = back[:, :, HEAD_SIZE:].transpose(1, 0, 2).reshape(home_rows, -1)

time: 377 us -> 200 us (0.53)
  blocking collectives: 191 us -> 0 us
  Pallas kernels: 9.56 us -> 91.4 us
  waiting for transfers between devices: 108 us -> 42.8 us
  between operations: 19.6 us -> 6.28 us
  local copies, waits for them, and re-layouts: 6.97 us -> 13.8 us
  starting transfers between devices: 30.1 us -> 36.8 us
    all_to_all x3 -> x0, blocking collectives: 191 us -> none  [the longest x1 154 us: per_device(): parts = exchange(dkv, 'seq')]
    pallas_call x0 -> x2, Pallas kernels: none -> 81.8 us  [the longest x1 50.6 us: reduce(): pl.pallas_call(reduce_kernel, name='reduce', out_shape=(jax.ShapeDtypeStr...]
    all_gather x1 -> x0, waiting for transfers between devices: 43.4 us -> none  [per_device(): all_kv = lax.all_gather(placed, 'seq', axis=0, tiled=False)]
    all_to_all x2, waiting for transfers between devices: 42.7 us -> 22.3 us  [the longest x1 13.1 us: per_device(): back = exchange(back.reshape(owners, 8, width), 'seq')]
    unnamed x11 -> x17, local copies, waits for them, and re-layouts: 2.05 us -> 8.21 us
    all_to_all x2, starting transfers between devices: 10 us -> 15.8 us  [the longest x1 8.18 us: per_device(): back = exchange(back.reshape(owners, 8, width), 'seq')]
  transfers between devices with their start and end apart: 5 -> 4, of which waited for: 5 -> 4; matrix products, arithmetic and copies ran while one was open for 1% -> 1% of each run, Pallas kernels for 0% -> 0%
where the time goes in v2:
time: 200 us; the launch traced here: 199 us
  Pallas kernels  91.4 us (46%)
  waiting for transfers between devices  42.8 us (21%)
  starting transfers between devices  36.8 us (18%)
  local copies, waits for them, and re-layouts  13.8 us (7%)
  other arithmetic  6.61 us (3%)
  between operations  6.28 us (3%)
    pallas_call x1, Pallas kernels, reduce(): pl.pallas_call(reduce_kernel, name='reduce', out_shape=(jax.ShapeDtypeStr...  50.6 us
    pallas_call x1, Pallas kernels, gather(): pl.pallas_call(gather_kernel, name='gather', out_shape=(jax.ShapeDtypeStr...  31.2 us
    all_to_all x1, starting transfers between devices, per_device(): arrived = exchange(jnp.concatenate([by_owner, tail], axis=1), 'seq')  16.7 us
    all_to_all x1, waiting for transfers between devices, per_device(): back = exchange(back.reshape(owners, 8, width), 'seq')  13.1 us
    all_to_all x1, waiting for transfers between devices, per_device(): arrived = exchange(jnp.concatenate([by_owner, tail], axis=1), 'seq')  11.8 us
    pallas_call x1, Pallas kernels, attention(): pl.pallas_call(attention_kernel, name='attention', out_shape=(jax.ShapeDt...  9.6 us
    all_to_all x1, waiting for transfers between devices, per_device(): first_pack = exchange(first_pack, 'head')  9.22 us
    all_to_all x1, waiting for transfers between devices, per_device(): back = exchange(back, 'head')  8.75 us
  transfers between devices with their start and end apart: 4, of which 4 were waited for; matrix products, arithmetic and copies ran while one was open for 1% of the time, Pallas kernels for 0%

profile of v2, /device:TPU:1, one launch (start us, length us, event | category | flops | bytes accessed | tf_op | source)
XLA Modules:
  0.0 198.9 jit_solution(1644345623069601864)
XLA Ops:
  0.6 1.3 fusion.33
  5.2 0.7 reshape.156
  5.9 0.9 copy.59
  6.8 0.9 copy.60
  7.7 1.3 multiply_bitcast_fusion
  9.2 0.3 reduce_sum.27
  9.8 0.8 copy.43
  10.6 7.6 %all-to-all-start = ((bf16[8,64,256]{2,1,0:T(8,128)(2,1)}), bf16[8,64,256]{2,1,0:T(8,128)(2,1)S(1)}, u32[]{:S(2)}, u32[]{:S(2)}) async-start(bf16[8,64,256]{2,1,0:T(8,128)(2,1)} %copy.43), calls=%async_computation | async-start | bytes 524288 | tf_op jit(solution)/shard_map/all_to_all | solution.py:384
  18.4 9.2 %all-to-all-done = bf16[8,64,256]{2,1,0:T(8,128)(2,1)S(1)} async-done(((bf16[8,64,256]{2,1,0:T(8,128)(2,1)}), bf16[8,64,256]{2,1,0:T(8,128)(2,1)S(1)}, u32[]{:S(2)}, u32[]{:S(2)}) %all-to-all-start) | async-done | bytes 262176 | tf_op jit(solution)/shard_map/all_to_all | solution.py:384
  27.7 0.7 slice_reduce_fusion
  29.0 0.6 fusion.34
  31.5 0.9 copy.44
  32.3 16.7 %all-to-all-start.1 = ((bf16[64,8,256]{2,1,0:T(8,128)(2,1)}), bf16[64,8,256]{2,1,0:T(8,128)(2,1)S(1)}, u32[]{:S(2)}, u32[]{:S(2)}) async-start(bf16[64,8,256]{2,1,0:T(8,128)(2,1)} %copy.44), calls=%async_computation.1 | async-start | bytes 524288 | tf_op jit(solution)/shard_map/all_to_all | solution.py:401
  49.1 0.7 pad_add_fusion.meta_ref
  49.7 0.6 slice_bitcast_fusion.3
  50.3 11.8 %all-to-all-done.1 = bf16[64,8,256]{2,1,0:T(8,128)(2,1)S(1)} async-done(((bf16[64,8,256]{2,1,0:T(8,128)(2,1)}), bf16[64,8,256]{2,1,0:T(8,128)(2,1)S(1)}, u32[]{:S(2)}, u32[]{:S(2)}) %all-to-all-start.1) | async-done | bytes 262176 | tf_op jit(solution)/shard_map/all_to_all | solution.py:401
  63.0 31.2 %gather.1 = (bf16[2,8,4,128,256]{4,3,2,1,0:T(8,128)(2,1)S(1)}, bf16[8,48,1280]{2,1,0:T(8,128)(2,1)S(1)}) custom-call(bf16[128,256]{1,0:T(8,128)(2,1)S(1)} %convolution_convert_fusion.1.own_ref, bf16[8,48,1280]{2,1,0:T(8,128)(2,1)S(1)} %pad_maximum_fusion.qd_ref), custom_call_target="tpu_custom_call" | custom-call | tf_op jit(solution)/shard_map/gather/pallas_call | solution.py:233
  94.2 1.9 copy-done.2
  96.1 1.0 copy-done.3
  97.2 9.6 %attention.1 = (bf16[384,640]{1,0:T(8,128)(2,1)}, bf16[64,128,256]{2,1,0:T(8,128)(2,1)}) custom-call(s32[2]{0:T(128)} %pad_add_fusion.meta_ref, bf16[384,1280]{1,0:T(8,128)(2,1)} %bitcast.89, f32[3,640]{1,0:T(4,128)} %get-tuple-element.23.lse_ref, f32[3,640]{1,0:T(4,128)} %get-tuple-element.22.delta_ref, bf16[64,128,256]{2,1,0:T(8,128)(2,1)} %bitcast.88), custom_call_target="tpu_custom_call" | custom-call | flops 10066329600 | bytes 11337728 | tf_op jit(solution)/shard_map/attention/pallas_call | solution.py:111
  106.8 2.2 %copy-done = bf16[64,128,256]{2,1,0:T(8,128)(2,1)S(1)} copy-done((bf16[64,128,256]{2,1,0:T(8,128)(2,1)S(1)}, bf16[64,128,256]{2,1,0:T(8,128)(2,1)}, u32[]{:S(2)}) %copy-start) | copy-done | bytes 4194328
  108.9 1.0 copy-done.1
  110.0 50.6 %reduce.8 = (bf16[128,256]{1,0:T(8,128)(2,1)S(1)}, bf16[8,48,640]{2,1,0:T(8,128)(2,1)S(1)}) custom-call(bf16[2,8,4,128,256]{4,3,2,1,0:T(8,128)(2,1)S(1)} %bitcast.85, bf16[8,48,640]{2,1,0:T(8,128)(2,1)S(1)} %bitcast.87), custom_call_target="tpu_custom_call" | custom-call | tf_op jit(solution)/shard_map/reduce/pallas_call | solution.py:328
  160.6 1.0 fusion
  161.6 8.2 %all-to-all-start.2 = ((bf16[64,8,256]{2,1,0:T(8,128)(2,1)}), bf16[64,8,256]{2,1,0:T(8,128)(2,1)S(1)}, u32[]{:S(2)}, u32[]{:S(2)}) async-start(bf16[64,8,256]{2,1,0:T(8,128)(2,1)} %fusion), calls=%async_computation.2 | async-start | bytes 524288 | tf_op jit(solution)/shard_map/all_to_all | solution.py:434
  169.8 13.1 %all-to-all-done.2 = bf16[64,8,256]{2,1,0:T(8,128)(2,1)S(1)} async-done(((bf16[64,8,256]{2,1,0:T(8,128)(2,1)}), bf16[64,8,256]{2,1,0:T(8,128)(2,1)S(1)}, u32[]{:S(2)}, u32[]{:S(2)}) %all-to-all-start.2) | async-done | bytes 262176 | tf_op jit(solution)/shard_map/all_to_all | solution.py:434
  182.9 0.8 fusion.7
  183.7 4.2 %all-to-all-start.3 = ((bf16[8,48,256]{2,1,0:T(8,128)(2,1)}), bf16[8,48,256]{2,1,0:T(8,128)(2,1)S(1)}, u32[]{:S(2)}, u32[]{:S(2)}) async-start(bf16[8,48,256]{2,1,0:T(8,128)(2,1)} %bitcast.32), calls=%async_computation.3 | async-start | bytes 393216 | tf_op jit(solution)/shard_map/all_to_all | solution.py:437
  188.0 0.8 copy.56
  188.8 8.8 %all-to-all-done.3 = bf16[8,48,256]{2,1,0:T(8,128)(2,1)S(1)} async-done(((bf16[8,48,256]{2,1,0:T(8,128)(2,1)}), bf16[8,48,256]{2,1,0:T(8,128)(2,1)S(1)}, u32[]{:S(2)}, u32[]{:S(2)}) %all-to-all-start.3) | async-done | bytes 196640 | tf_op jit(solution)/shard_map/all_to_all | solution.py:437
  197.6 0.7 copy.69
  198.3 0.7 copy.70
  (42 shorter events, 1.9 us)
Async XLA Ops:
  9.0 9.2 %copy-start.4 = (bf16[48,5120]{1,0:T(8,128)(2,1)S(1)}, bf16[48,5120]{1,0:T(8,128)(2,1)}, u32[]{:S(2)}) copy-start(bf16[48,5120]{1,0:T(8,128)(2,1)} %param.11) | copy-start | bytes 1474564
  9.0 9.2 %copy-start.5 = (bf16[48,5120]{1,0:T(8,128)(2,1)S(1)}, bf16[48,5120]{1,0:T(8,128)(2,1)}, u32[]{:S(2)}) copy-start(bf16[48,5120]{1,0:T(8,128)(2,1)} %param.7) | copy-start | bytes 1474564
  10.6 17.1 %all-to-all-start = ((bf16[8,64,256]{2,1,0:T(8,128)(2,1)}), bf16[8,64,256]{2,1,0:T(8,128)(2,1)S(1)}, u32[]{:S(2)}, u32[]{:S(2)}) async-start(bf16[8,64,256]{2,1,0:T(8,128)(2,1)} %copy.43), calls=%async_computation | async-start | bytes 524288 | tf_op jit(solution)/shard_map/all_to_all | solution.py:384
  32.3 29.8 %all-to-all-start.1 = ((bf16[64,8,256]{2,1,0:T(8,128)(2,1)}), bf16[64,8,256]{2,1,0:T(8,128)(2,1)S(1)}, u32[]{:S(2)}, u32[]{:S(2)}) async-start(bf16[64,8,256]{2,1,0:T(8,128)(2,1)} %copy.44), calls=%async_computation.1 | async-start | bytes 524288 | tf_op jit(solution)/shard_map/all_to_all | solution.py:401
  94.2 1.9 copy-start.2
  96.1 1.0 copy-start.3
  106.8 2.2 %copy-start = (bf16[64,128,256]{2,1,0:T(8,128)(2,1)S(1)}, bf16[64,128,256]{2,1,0:T(8,128)(2,1)}, u32[]{:S(2)}) copy-start(bf16[64,128,256]{2,1,0:T(8,128)(2,1)} %get-tuple-element.11) | copy-start | bytes 12582916
  108.9 1.0 copy-start.1
  161.6 21.3 %all-to-all-start.2 = ((bf16[64,8,256]{2,1,0:T(8,128)(2,1)}), bf16[64,8,256]{2,1,0:T(8,128)(2,1)S(1)}, u32[]{:S(2)}, u32[]{:S(2)}) async-start(bf16[64,8,256]{2,1,0:T(8,128)(2,1)} %fusion), calls=%async_computation.2 | async-start | bytes 524288 | tf_op jit(solution)/shard_map/all_to_all | solution.py:434
  183.7 13.8 %all-to-all-start.3 = ((bf16[8,48,256]{2,1,0:T(8,128)(2,1)}), bf16[8,48,256]{2,1,0:T(8,128)(2,1)S(1)}, u32[]{:S(2)}, u32[]{:S(2)}) async-start(bf16[8,48,256]{2,1,0:T(8,128)(2,1)} %bitcast.32), calls=%async_computation.3 | async-start | bytes 393216 | tf_op jit(solution)/shard_map/all_to_all | solution.py:437

commit v3 on v2

--- a/solution.py
+++ b/solution.py
@@ -1,5 +1,3 @@
-import functools
-
 import jax
 import jax.numpy as jnp
 from jax import lax
@@ -151,7 +149,20 @@
 
 def meet(groups):
     barrier = pltpu.get_barrier_semaphore()
-    total = 0
+    seq = lax.axis_index("seq")
+    head = lax.axis_index("head")
+
+    def greet(k, carry):
+        pl.semaphore_signal(
+            barrier,
+            inc=1,
+            device_id=((seq + k) % 64, head),
+            device_id_type=pl.DeviceIdType.MESH,
+        )
+        return carry
+
+    lax.fori_loop(1, 64, greet, 0)
+    total = 63
     for group in groups:
         for device in group:
             pl.semaphore_signal(
@@ -172,30 +183,147 @@
     )
 
 
+def scatter_seq(out_ref, in_ref, own_sem, send, recv):
+    seq = lax.axis_index("seq")
+    head = lax.axis_index("head")
+    own = pltpu.make_async_copy(out_ref.at[seq], in_ref.at[seq], own_sem)
+    own.start()
+
+    def copy(k):
+        there = (seq + k) % 64
+        return remote(
+            out_ref.at[there], in_ref.at[seq], send.at[k], recv.at[k], (there, head)
+        )
+
+    def start(k, carry):
+        copy(k).start()
+        return carry
+
+    def finish(k, carry):
+        from_there = in_ref.at[(seq + 64 - k) % 64]
+        arrived = remote(
+            from_there, from_there, send.at[k], recv.at[k], ((seq + k) % 64, head)
+        )
+        arrived.wait_recv()
+        return carry
+
+    def sent(k, carry):
+        copy(k).wait_send()
+        return carry
+
+    lax.fori_loop(1, 64, start, 0)
+    lax.fori_loop(1, 64, finish, 0)
+    own.wait()
+    return lambda: lax.fori_loop(1, 64, sent, 0)
+
+
+def scatter_head(out_ref, in_ref, head, own_sem, send, recv, to_head):
+    copies = []
+    for d in NEAR_FIRST[1:]:
+        copy = remote(
+            out_ref.at[(head + d) % 8], in_ref.at[head], send.at[d], recv.at[d], to_head[d]
+        )
+        copy.start()
+        copies.append(copy)
+    own = pltpu.make_async_copy(out_ref.at[head], in_ref.at[head], own_sem)
+    own.start()
+
+    def finish():
+        for d in NEAR_FIRST[1:]:
+            part = in_ref.at[(head + 8 - d) % 8]
+            remote(part, part, send.at[d], recv.at[d], to_head[d]).wait_recv()
+        own.wait()
+
+    return copies, finish
+
+
+def wide(value, shape):
+    return jnp.broadcast_to(value, shape)
+
+
 NEAR_FIRST = (0, 1, 7, 2, 6, 3, 5, 4)
 
 
 def gather_kernel(
-    own_ref, qd_ref, kv_ref, rows_ref, own_sem, z_send, z_recv, x_send, x_recv, p_send, p_recv,
-    h_send, h_recv,
+    pack_ref, qd_ref, kv_ref, rows_ref, got_ref, pick_ref, to_owner, at_owner, own_ref, own_sem,
+    z_send, z_recv, x_send, x_recv, p_send, p_recv, h_send, h_recv, k_send, k_recv, s_send, s_recv,
 ):
     z, x, core, head, to_z, to_x, partner, to_head = peers()
-    meet((to_z[1:], to_x[1:], (partner,), to_head[1:]))
-    copies = []
+    f32 = jnp.float32
+    i32 = jnp.int32
+    bf16 = jnp.bfloat16
+    meet((to_head[1:],))
+    copies, arrive = scatter_head(
+        pack_ref, got_ref, head, own_sem.at[0], k_send, k_recv, to_head
+    )
+    arrive()
+    more, arrive_rows = scatter_head(
+        qd_ref, rows_ref, head, own_sem.at[1], h_send, h_recv, to_head
+    )
+    copies = copies + more
+    home = got_ref.shape[1] - 16
+    capacity = 8 * home
+    slots = capacity // 64
+    notes = got_ref[0, pl.ds(home, 16), :].astype(f32)
+    first = (notes[10:11, 0:1] * 128 + notes[10:11, 1:2]).astype(i32)
+    count = notes[10:11, 2:3]
+    for h in range(1, 8):
+        count = count + got_ref[h, pl.ds(home, 16), :].astype(f32)[10:11, 2:3]
+    count = count.astype(i32)
+    shape = (1024, capacity)
+    row = lax.broadcasted_iota(i32, shape, 0)
+    column = lax.broadcasted_iota(i32, shape, 1)
+    wanted = (row % 8) * 64 + ((row // 16 - wide(first, shape)) & 63)
+    hit = (column == wanted) & (row % 8 < slots)
+    is_key = (row // 8) % 2 == 0
+    one = jnp.ones((), f32)
+    zero = jnp.zeros((), f32)
+    take_key = jnp.where(hit & is_key, one, zero).astype(bf16)
+    take_value = jnp.where(hit & ~is_key, one, zero).astype(bf16)
+    pairs = got_ref[:, pl.ds(0, home), :].reshape(capacity, 2 * HEAD_SIZE)
+    sent = jnp.dot(take_key, pairs[:, :HEAD_SIZE], preferred_element_type=f32) + jnp.dot(
+        take_value, pairs[:, HEAD_SIZE:], preferred_element_type=f32
+    )
+    shape = (1024, HEAD_SIZE)
+    row = lax.broadcasted_iota(i32, shape, 0)
+    lane = lax.broadcasted_iota(i32, shape, 1)
+    first_wide = wide(first, shape)
+    count_wide = wide(count, shape)
+    note = jnp.where(
+        lane == 0,
+        first_wide >> 7,
+        jnp.where(
+            lane == 1,
+            first_wide & 127,
+            jnp.where(lane == 2, count_wide >> 7, jnp.where(lane == 3, count_wide & 127, 0)),
+        ),
+    ).astype(f32)
+    sent = jnp.where(row % 16 == slots, note, sent)
+    to_owner[...] = sent.astype(bf16).reshape(64, 16, HEAD_SIZE)
+    drain = scatter_seq(to_owner, at_owner, own_sem.at[2], s_send, s_recv)
+    come = at_owner[...].reshape(1024, HEAD_SIZE)
+    told = come.astype(f32).reshape(64, 16, HEAD_SIZE)[:, slots : slots + 1, :]
+    told = wide(told, (64, 16, HEAD_SIZE)).reshape(1024, HEAD_SIZE)
+    starts = wide((told[:, 0:1] * 128 + told[:, 1:2]).astype(i32), shape)
+    counts = wide((told[:, 2:3] * 128 + told[:, 3:4]).astype(i32), shape)
+    turn = row % 8
+    within = turn * 64 + ((lax.axis_index("seq") - starts) & 63)
+    alive = (within < counts) & (turn < slots)
+    target = jnp.where(alive, (starts + within) >> 6, -1)
+    pick = jnp.where(target == lane, one, zero)
+    pick_ref[...] = pick.astype(bf16)
+    is_key = (row // 8) % 2 == 0
+    for half in range(2):
+        chosen = jnp.where(is_key if half == 0 else ~is_key, pick, zero).T.astype(bf16)
+        own_ref[:, pl.ds(half * HEAD_SIZE, HEAD_SIZE)] = jnp.dot(
+            chosen, come, preferred_element_type=f32
+        ).astype(bf16)
     for d in NEAR_FIRST[1:]:
         copy = remote(own_ref, kv_ref.at[core, z, x], z_send.at[d], z_recv.at[d], to_z[d])
         copy.start()
         copies.append(copy)
-    for d in NEAR_FIRST[1:]:
-        copy = remote(
-            qd_ref.at[(head + d) % 8], rows_ref.at[head], h_send.at[d], h_recv.at[d], to_head[d]
-        )
-        copy.start()
-        copies.append(copy)
-    mine = pltpu.make_async_copy(own_ref, kv_ref.at[core, z, x], own_sem.at[0])
+    mine = pltpu.make_async_copy(own_ref, kv_ref.at[core, z, x], own_sem.at[3])
     mine.start()
-    kept = pltpu.make_async_copy(qd_ref.at[head], rows_ref.at[head], own_sem.at[1])
-    kept.start()
     for d in NEAR_FIRST:
         source = (z + 8 - d) % 8
         block = kv_ref.at[core, source, x]
@@ -219,43 +347,47 @@
     for d in NEAR_FIRST:
         row = kv_ref.at[1 - core, (z + 8 - d) % 8]
         remote(row, row, p_send.at[d], p_recv.at[d], partner).wait_recv()
-    for d in NEAR_FIRST[1:]:
-        part = rows_ref.at[(head + 8 - d) % 8]
-        remote(part, part, h_send.at[d], h_recv.at[d], to_head[d]).wait_recv()
-    kept.wait()
+    arrive_rows()
+    drain()
     for copy in copies:
         copy.wait_send()
 
 
-def gather(own, qd):
+def gather(pack, qd):
     vmem = pl.BlockSpec(memory_space=pltpu.VMEM)
     dma = pltpu.SemaphoreType.DMA
     return pl.pallas_call(
         gather_kernel,
         name="gather",
         out_shape=(
-            jax.ShapeDtypeStruct((2, 8, 4) + own.shape, own.dtype),
+            jax.ShapeDtypeStruct((2, 8, 4, BALANCED_TOKENS, 2 * HEAD_SIZE), pack.dtype),
             jax.ShapeDtypeStruct(qd.shape, qd.dtype),
+            jax.ShapeDtypeStruct(pack.shape, pack.dtype),
+            jax.ShapeDtypeStruct((1024, BALANCED_TOKENS), pack.dtype),
         ),
         in_specs=[vmem, vmem],
-        out_specs=(vmem, vmem),
+        out_specs=(vmem,) * 4,
         scratch_shapes=[
-            dma((2,)), dma((8,)), dma((8,)), dma((8, 4)), dma((8, 4)), dma((8,)), dma((8,)),
-            dma((8,)), dma((8,)),
+            pltpu.VMEM((64, 16, HEAD_SIZE), pack.dtype),
+            pltpu.VMEM((64, 16, HEAD_SIZE), pack.dtype),
+            pltpu.VMEM((BALANCED_TOKENS, 2 * HEAD_SIZE), pack.dtype),
+            dma((4,)), dma((8,)), dma((8,)), dma((8, 4)), dma((8, 4)), dma((8,)), dma((8,)),
+            dma((8,)), dma((8,)), dma((8,)), dma((8,)), dma((64,)), dma((64,)),
         ],
         compiler_params=pltpu.CompilerParams(
-            collective_id=0, has_side_effects=True, vmem_limit_bytes=32 << 20
-        ),
-    )(own, qd)
+            collective_id=0, has_side_effects=True, vmem_limit_bytes=48 << 20
+        ),
+    )(pack, qd)
 
 
 def reduce_kernel(
-    kv_ref, dq_ref, sum_ref, rows_ref, from_core, to_row, from_row, to_column, from_column, total,
-    own_sem, p_send, p_recv, x_send, x_recv, z_send, z_recv, h_send, h_recv,
+    first_ref, pick_ref, kv_ref, dq_ref, grad_ref, rows_ref, from_core, to_row, from_row, to_column,
+    from_column, total, to_home, at_home, to_slot, own_sem, p_send, p_recv, x_send, x_recv, z_send,
+    z_recv, h_send, h_recv, k_send, k_recv, s_send, s_recv,
 ):
     z, x, core, head, to_z, to_x, partner, to_head = peers()
     f32 = jnp.float32
-    meet((to_z[1:], to_x[1:], (partner,), to_head[1:]))
+    meet((to_head[1:],))
     order = (4, 3, 5, 2, 6, 1, 7, 0)
     copies = []
     for d in order:
@@ -265,14 +397,10 @@
         )
         copy.start()
         copies.append(copy)
-    for d in NEAR_FIRST[1:]:
-        copy = remote(
-            dq_ref.at[(head + d) % 8], rows_ref.at[head], h_send.at[d], h_recv.at[d], to_head[d]
-        )
-        copy.start()
-        copies.append(copy)
-    kept = pltpu.make_async_copy(dq_ref.at[head], rows_ref.at[head], own_sem.at[0])
-    kept.start()
+    more, arrive_rows = scatter_head(
+        dq_ref, rows_ref, head, own_sem.at[0], h_send, h_recv, to_head
+    )
+    copies = copies + more
     for d in order:
         there = (z + d) % 8
         remote(
@@ -311,16 +439,45 @@
             to_column.at[d], from_column.at[d], z_send.at[d], z_recv.at[d], to_z[d]
         ).wait_recv()
         part = part + from_column[d].astype(f32)
-    sum_ref[...] = part.astype(sum_ref.dtype)
-    for d in NEAR_FIRST[1:]:
-        piece = rows_ref.at[(head + 8 - d) % 8]
-        remote(piece, piece, h_send.at[d], h_recv.at[d], to_head[d]).wait_recv()
-    kept.wait()
+    i32 = jnp.int32
+    bf16 = jnp.bfloat16
+    one = jnp.ones((), f32)
+    zero = jnp.zeros((), f32)
+    part = part.astype(bf16)
+    pick = pick_ref[...].astype(f32)
+    is_key = (lax.broadcasted_iota(i32, pick.shape, 0) // 8) % 2 == 0
+    sent = jnp.dot(
+        jnp.where(is_key, pick, zero).astype(bf16), part[:, :HEAD_SIZE], preferred_element_type=f32
+    ) + jnp.dot(
+        jnp.where(is_key, zero, pick).astype(bf16), part[:, HEAD_SIZE:], preferred_element_type=f32
+    )
+    to_home[...] = sent.astype(bf16).reshape(64, 16, HEAD_SIZE)
+    drain = scatter_seq(to_home, at_home, own_sem.at[1], s_send, s_recv)
+    home = to_slot.shape[1]
+    shape = (8 * home, 1024)
+    slot = lax.broadcasted_iota(i32, shape, 0)
+    column = lax.broadcasted_iota(i32, shape, 1)
+    wanted = (((slot & 63) + wide(first_ref[0:1, 0:1], shape)) & 63) * 16 + (slot >> 6)
+    come = at_home[...].reshape(1024, HEAD_SIZE)
+    for half in range(2):
+        chosen = jnp.where(column == wanted + 8 * half, one, zero).astype(bf16)
+        to_slot[:, :, pl.ds(half * HEAD_SIZE, HEAD_SIZE)] = (
+            jnp.dot(chosen, come, preferred_element_type=f32)
+            .astype(bf16)
+            .reshape(8, home, HEAD_SIZE)
+        )
+    more, arrive = scatter_head(
+        to_slot, grad_ref, head, own_sem.at[2], k_send, k_recv, to_head
+    )
+    copies = copies + more
+    arrive_rows()
+    arrive()
+    drain()
     for copy in copies:
         copy.wait_send()
 
 
-def reduce(dkv, dq):
+def reduce(first, pick, dkv, dq):
     vmem = pl.BlockSpec(memory_space=pltpu.VMEM)
     dma = pltpu.SemaphoreType.DMA
     block = dkv.shape[3:]
@@ -329,10 +486,10 @@
         reduce_kernel,
         name="reduce",
         out_shape=(
-            jax.ShapeDtypeStruct(block, bf16),
+            jax.ShapeDtypeStruct(dq.shape[:2] + (2 * HEAD_SIZE,), bf16),
             jax.ShapeDtypeStruct(dq.shape, dq.dtype),
         ),
-        in_specs=[vmem, vmem],
+        in_specs=[vmem] * 4,
         out_specs=(vmem, vmem),
         scratch_shapes=[
             pltpu.VMEM((8, 4) + block, bf16),
@@ -341,26 +498,26 @@
             pltpu.VMEM((8,) + block, bf16),
             pltpu.VMEM((8,) + block, bf16),
             pltpu.VMEM(block, jnp.float32),
-            dma((1,)), dma((8,)), dma((8,)), dma((4, 8)), dma((4, 8)), dma((8,)), dma((8,)),
-            dma((8,)), dma((8,)),
+            pltpu.VMEM((64, 16, HEAD_SIZE), bf16),
+            pltpu.VMEM((64, 16, HEAD_SIZE), bf16),
+            pltpu.VMEM(dq.shape[:2] + (2 * HEAD_SIZE,), bf16),
+            dma((3,)), dma((8,)), dma((8,)), dma((4, 8)), dma((4, 8)), dma((8,)), dma((8,)),
+            dma((8,)), dma((8,)), dma((8,)), dma((8,)), dma((64,)), dma((64,)),
         ],
         compiler_params=pltpu.CompilerParams(
             collective_id=1, has_side_effects=True, vmem_limit_bytes=40 << 20
         ),
-    )(dkv, dq)
+    )(first, pick, dkv, dq)
 
 
 def per_device(queries, keys, values, outputs, output_gradient, lse, ranks):
     owners = lax.axis_size("seq")
     heads = lax.axis_size("head")
-    me = lax.axis_index("seq")
     home_rows = queries.shape[0]
     capacity = home_rows * heads
-    slots = capacity // owners
     survivors = BALANCED_TOKENS * owners
     bf16 = jnp.bfloat16
     width = 2 * HEAD_SIZE
-    exchange = functools.partial(lax.all_to_all, split_axis=0, concat_axis=0, tiled=True)
 
     dots = jnp.sum(
         output_gradient.astype(jnp.float32).reshape(home_rows, QUERY_HEADS, HEAD_SIZE)
@@ -381,37 +538,13 @@
     first_pack = jnp.concatenate(
         [jnp.concatenate([by_head(keys), by_head(values)], axis=-1), small, digit_rows], axis=1
     )
-    first_pack = exchange(first_pack, "head")
-    pairs = first_pack[:, :home_rows].reshape(slots, owners, width)
+    all_kv, qd, first_pack, pick = gather(
+        first_pack, jnp.concatenate([by_head(queries), by_head(output_gradient)], axis=-1)
+    )
     extra = first_pack[:, home_rows:].astype(jnp.float32)
     first_rank = (extra[0, 2 * GROUP, 0] * 128 + extra[0, 2 * GROUP, 1]).astype(jnp.int32)
     count = jnp.sum(extra[:, 2 * GROUP, 2]).astype(jnp.int32)
 
-    turn = first_rank % owners
-    by_owner = pairs.transpose(1, 0, 2)
-    by_owner = lax.dynamic_slice_in_dim(
-        jnp.concatenate([by_owner, by_owner], axis=0), owners - turn, owners, 0
-    )
-    head_digits = jnp.stack(
-        [first_rank // 128, first_rank % 128, count // 128, count % 128]
-    ).astype(bf16)
-    tail = jnp.broadcast_to(
-        jnp.pad(head_digits, (0, width - 4))[None, None], (owners, 8 - slots, width)
-    )
-    arrived = exchange(jnp.concatenate([by_owner, tail], axis=1), "seq")
-    told = arrived[:, slots].astype(jnp.float32)
-    starts = (told[:, 0] * 128 + told[:, 1]).astype(jnp.int32)
-    counts = (told[:, 2] * 128 + told[:, 3]).astype(jnp.int32)
-    within = jnp.arange(8, dtype=jnp.int32)[None, :] * owners + ((me - starts) % owners)[:, None]
-    alive = (within < counts[:, None]) & (jnp.arange(8) < slots)[None, :]
-    target = jnp.where(alive, (starts[:, None] + within) // owners, -1).reshape(-1)
-    pick = (target[None, :] == jnp.arange(BALANCED_TOKENS, dtype=jnp.int32)[:, None]).astype(bf16)
-    placed = jnp.dot(
-        pick, arrived.reshape(owners * 8, width), preferred_element_type=jnp.float32
-    ).astype(bf16)
-    all_kv, qd = gather(
-        placed, jnp.concatenate([by_head(queries), by_head(output_gradient)], axis=-1)
-    )
     all_kv = all_kv.reshape(owners, BALANCED_TOKENS, width)
     qd = qd.reshape(capacity, 2 * GROUP * HEAD_SIZE)
 
@@ -424,17 +557,12 @@
         jnp.stack([first_rank, count]), qd, per_row[0] * LOG2E, per_row[1], all_kv
     )
 
-    summed, dq = reduce(
+    back, dq = reduce(
+        jnp.broadcast_to(first_rank, (8, HEAD_SIZE)),
+        pick,
         dkv.reshape(2, 8, 4, BALANCED_TOKENS, width),
         dq.reshape(heads, home_rows, GROUP * HEAD_SIZE),
     )
-    back = lax.dot_general(
-        pick, summed, (((0,), (0,)), ((), ())), preferred_element_type=jnp.float32
-    ).astype(bf16)
-    back = exchange(back.reshape(owners, 8, width), "seq")
-    back = lax.dynamic_slice_in_dim(jnp.concatenate([back, back], axis=0), turn, owners, 0)
-    back = back[:, :slots].transpose(1, 0, 2).reshape(heads, home_rows, width)
-    back = exchange(back, "head")
     query_grads = dq.transpose(1, 0, 2).reshape(home_rows, -1)
     key_grads = back[:, :, :HEAD_SIZE].transpose(1, 0, 2).reshape(home_rows, -1)
     value_grads = back[:, :, HEAD_SIZE:].transpose(1, 0, 2).reshape(home_rows, -1)

time: 200 us -> 171 us (0.85)
  Pallas kernels: 91.4 us -> 150 us
  waiting for transfers between devices: 42.8 us -> 0 us
  starting transfers between devices: 36.8 us -> 0 us
  local copies, waits for them, and re-layouts: 13.8 us -> 9.58 us
    all_to_all x4 -> x0, waiting for transfers between devices: 42.8 us -> none  [the longest x1 13.1 us: per_device(): back = exchange(back.reshape(owners, 8, width), 'seq')]
    pallas_call x1, Pallas kernels: 31.2 us -> 68.7 us  [gather(): pl.pallas_call(gather_kernel, name='gather', out_shape=(jax.ShapeDtypeStr...]
    all_to_all x4 -> x0, starting transfers between devices: 36.8 us -> none  [the longest x1 16.7 us: per_device(): arrived = exchange(jnp.concatenate([by_owner, tail], axis=1), 'seq')]
    pallas_call x1, Pallas kernels: 50.6 us -> 72 us  [reduce(): pl.pallas_call(reduce_kernel, name='reduce', out_shape=(jax.ShapeDtypeStr...]
    unnamed x17 -> x14, local copies, waits for them, and re-layouts: 8.21 us -> 4.9 us
  transfers between devices with their start and end apart: 4 -> 0, of which waited for: 4 -> 0; matrix products, arithmetic and copies ran while one was open for 1% -> 0% of each run, Pallas kernels for 0% -> 0%
where the time goes in v3:
time: 171 us
  Pallas kernels  150 us (88%)
  local copies, waits for them, and re-layouts  9.58 us (6%)
  between operations  6.02 us (4%)
  other arithmetic  5.13 us (3%)
    pallas_call x1, Pallas kernels, reduce(): pl.pallas_call(reduce_kernel, name='reduce', out_shape=(jax.ShapeDtypeStr...  72 us
    pallas_call x1, Pallas kernels, gather(): pl.pallas_call(gather_kernel, name='gather', out_shape=(jax.ShapeDtypeStr...  68.7 us
    pallas_call x1, Pallas kernels, attention(): pl.pallas_call(attention_kernel, name='attention', out_shape=(jax.ShapeDt...  9.6 us
    unnamed x14, local copies, waits for them, and re-layouts  4.9 us

profile of v3, /device:TPU:1, one launch (start us, length us, event | category | flops | bytes accessed | tf_op | source)
XLA Modules:
  0.0 171.0 jit_solution(3689425460367092145)
XLA Ops:
  0.6 0.0 copy-start
  0.6 1.3 fusion.10
  5.2 0.1 fusion.9
  5.3 0.7 reshape.78
  6.1 0.0 copy-done
  6.1 0.9 bitcast_bitcast_fusion.2
  7.0 1.3 multiply_bitcast_fusion
  8.3 0.0 copy-start.4
  8.3 0.0 copy-start.5
  8.3 0.2 copy.43
  8.5 0.3 reduce_sum.27
  8.8 0.1 copy.29
  9.0 0.3 copy-done.4
  9.3 0.1 copy-done.5
  9.5 0.1 bitcast_bitcast_fusion
  9.5 0.1 pad_maximum_fusion.qd_ref
  9.6 68.7 %gather.1 = (bf16[2,8,4,128,256]{4,3,2,1,0:T(8,128)(2,1)}, bf16[8,48,1280]{2,1,0:T(8,128)(2,1)S(1)}, bf16[8,64,256]{2,1,0:T(8,128)(2,1)S(1)}, bf16[1024,128]{1,0:T(8,128)(2,1)S(1)}) custom-call(bf16[8,64,256]{2,1,0:T(8,128)(2,1)S(1)} %fusion.3.pack_ref, bf16[8,48,1280]{2,1,0:T(8,128)(2,1)S(1)} %pad_maximum_fusion.qd_ref), custom_call_target="tpu_custom_call" | custom-call | tf_op jit(solution)/shard_map/gather/pallas_call | solution.py:359
  78.3 0.0 copy-start.3
  78.3 1.0 copy-done.3
  79.3 0.7 slice_reduce_fusion
  80.7 0.6 fusion.11
  82.6 0.1 reshape.82
  82.7 0.7 pad_add_fusion.meta_ref
  83.4 0.6 slice_bitcast_fusion.3
  84.0 9.6 %attention.1 = (bf16[384,640]{1,0:T(8,128)(2,1)}, bf16[64,128,256]{2,1,0:T(8,128)(2,1)}) custom-call(s32[2]{0:T(128)} %pad_add_fusion.meta_ref, bf16[384,1280]{1,0:T(8,128)(2,1)} %bitcast.73, f32[3,640]{1,0:T(4,128)} %get-tuple-element.24.lse_ref, f32[3,640]{1,0:T(4,128)} %get-tuple-element.23.delta_ref, bf16[64,128,256]{2,1,0:T(8,128)(2,1)} %bitcast.86), custom_call_target="tpu_custom_call" | custom-call | flops 10066329600 | bytes 11337728 | tf_op jit(solution)/shard_map/attention/pallas_call | solution.py:109
  93.6 0.0 copy-start.1
  93.6 2.2 %copy-done.1 = bf16[64,128,256]{2,1,0:T(8,128)(2,1)S(1)} copy-done((bf16[64,128,256]{2,1,0:T(8,128)(2,1)S(1)}, bf16[64,128,256]{2,1,0:T(8,128)(2,1)}, u32[]{:S(2)}) %copy-start.1) | copy-done | bytes 4194328
  95.8 1.0 copy-done.2
  96.8 72.0 %reduce.2 = (bf16[8,48,256]{2,1,0:T(8,128)(2,1)S(1)}, bf16[8,48,640]{2,1,0:T(8,128)(2,1)S(1)}) custom-call(s32[8,128]{1,0:T(8,128)S(1)} %broadcast_in_dim.23.first_ref, bf16[1024,128]{1,0:T(8,128)(2,1)S(1)} %get-tuple-element.12.pick_ref, bf16[2,8,4,128,256]{4,3,2,1,0:T(8,128)(2,1)S(1)} %bitcast.70, bf16[8,48,640]{2,1,0:T(8,128)(2,1)S(1)} %bitcast.72), custom_call_target="tpu_custom_call" | custom-call | tf_op jit(solution)/shard_map/reduce/pallas_call | solution.py:485
  168.8 0.8 copy.40
  169.6 0.7 copy.50
  170.3 0.7 copy.51
  (12 shorter events, 0.2 us)
Async XLA Ops:
  0.6 5.4 %copy-start = (bf16[48,1024]{1,0:T(8,128)(2,1)S(1)}, bf16[48,1024]{1,0:T(8,128)(2,1)}, u32[]{:S(2)}) copy-start(bf16[48,1024]{1,0:T(8,128)(2,1)} %param.8) | copy-start | bytes 294916
  8.3 1.0 copy-start.4
  8.3 1.2 copy-start.5
  78.3 1.0 copy-start.3
  93.6 2.2 %copy-start.1 = (bf16[64,128,256]{2,1,0:T(8,128)(2,1)S(1)}, bf16[64,128,256]{2,1,0:T(8,128)(2,1)}, u32[]{:S(2)}) copy-start(bf16[64,128,256]{2,1,0:T(8,128)(2,1)} %get-tuple-element.15) | copy-start | bytes 12582916
  95.8 1.0 copy-start.2

commit v4 on v3

--- a/solution.py
+++ b/solution.py
@@ -17,10 +17,10 @@
 
 
 def attention_kernel(
-    meta_ref, qd_ref, lse_ref, delta_ref, kv_ref, dq_ref, dkv_ref, q_sc, g_sc, dq_sc, acc
+    meta_ref, qd_ref, stat_ref, kv_ref, dq_ref, dkv_ref, q_sc, g_sc, dq_sc, acc
 ):
-    first = meta_ref[0]
-    count = meta_ref[1]
+    first = meta_ref[0, 0]
+    count = meta_ref[0, 1]
     owners = kv_ref.shape[0]
     blocks = q_sc.shape[0]
     stacked = GROUP * ROWS
@@ -70,10 +70,10 @@
                 limit = first + b * ROWS - j * row_span - (c % 2) * 32 - c // 2
                 prob = jnp.where(
                     gap <= limit,
-                    jnp.exp2(score * (scale * LOG2E) - lse_ref[pl.ds(b, 1), :]),
+                    jnp.exp2(score * (scale * LOG2E) - stat_ref[0, pl.ds(b, 1), :]),
                     0.0,
                 )
-                dscore = prob * (dprob - delta_ref[pl.ds(b, 1), :])
+                dscore = prob * (dprob - stat_ref[1, pl.ds(b, 1), :])
                 prob_low = prob.astype(jnp.bfloat16)
                 dscore_low = dscore.astype(jnp.bfloat16)
                 dk = lax.dot_general(dscore_low, q, nn, preferred_element_type=f32)
@@ -101,7 +101,7 @@
     )
 
 
-def attention(meta, qd, lse, delta, kv, interpret=False):
+def attention(meta, qd, stats, kv, interpret=False):
     capacity = qd.shape[0]
     owners, per_owner, width = kv.shape
     blocks = capacity // ROWS
@@ -113,7 +113,7 @@
             jax.ShapeDtypeStruct((capacity, GROUP * HEAD_SIZE), jnp.bfloat16),
             jax.ShapeDtypeStruct(kv.shape, jnp.bfloat16),
         ),
-        in_specs=[pl.BlockSpec(memory_space=pltpu.SMEM), vmem, vmem, vmem, vmem],
+        in_specs=[pl.BlockSpec(memory_space=pltpu.SMEM), vmem, vmem, vmem],
         out_specs=(vmem, vmem),
         scratch_shapes=[
             pltpu.VMEM((blocks, GROUP * ROWS, HEAD_SIZE), jnp.bfloat16),
@@ -121,14 +121,14 @@
             pltpu.VMEM((blocks, HEAD_SIZE, GROUP * ROWS), jnp.float32),
             pltpu.VMEM(kv.shape, jnp.float32),
         ],
-        compiler_params=pltpu.CompilerParams(vmem_limit_bytes=56 << 20),
+        compiler_params=pltpu.CompilerParams(vmem_limit_bytes=26 << 20),
         cost_estimate=pl.CostEstimate(
             flops=10 * capacity * GROUP * HEAD_SIZE * owners * per_owner // 2,
             bytes_accessed=2 * (2 * kv.size + 3 * qd.size),
             transcendentals=0,
         ),
         interpret=interpret,
-    )(meta, qd, lse, delta, kv)
+    )(meta, qd, stats, kv)
 
 
 def place(seq_index):
@@ -211,10 +211,12 @@
         copy(k).wait_send()
         return carry
 
+    def lands():
+        lax.fori_loop(1, 64, finish, 0)
+        own.wait()
+
     lax.fori_loop(1, 64, start, 0)
-    lax.fori_loop(1, 64, finish, 0)
-    own.wait()
-    return lambda: lax.fori_loop(1, 64, sent, 0)
+    return lands, lambda: lax.fori_loop(1, 64, sent, 0)
 
 
 def scatter_head(out_ref, in_ref, head, own_sem, send, recv, to_head):
@@ -245,7 +247,8 @@
 
 
 def gather_kernel(
-    pack_ref, qd_ref, kv_ref, rows_ref, got_ref, pick_ref, to_owner, at_owner, own_ref, own_sem,
+    pack_ref, qd_ref, kv_ref, rows_ref, meta_ref, stat_ref, pick_ref, got_ref, to_owner, at_owner,
+    own_ref, own_sem,
     z_send, z_recv, x_send, x_recv, p_send, p_recv, h_send, h_recv, k_send, k_recv, s_send, s_recv,
 ):
     z, x, core, head, to_z, to_x, partner, to_head = peers()
@@ -300,7 +303,31 @@
     ).astype(f32)
     sent = jnp.where(row % 16 == slots, note, sent)
     to_owner[...] = sent.astype(bf16).reshape(64, 16, HEAD_SIZE)
-    drain = scatter_seq(to_owner, at_owner, own_sem.at[2], s_send, s_recv)
+    lands, drain = scatter_seq(to_owner, at_owner, own_sem.at[2], s_send, s_recv)
+    shape = meta_ref.shape
+    lane_of = lax.broadcasted_iota(i32, shape, 1)
+    meta_ref[...] = jnp.where(
+        lane_of == 0, wide(first, shape), jnp.where(lane_of == 1, wide(count, shape), 0)
+    )
+    shape = (2 * HEAD_SIZE, capacity)
+    apart = lax.broadcasted_iota(i32, shape, 1) - lax.broadcasted_iota(i32, shape, 0)
+    inside = lax.broadcasted_iota(i32, shape, 0) < home
+    stats = jnp.zeros((16, capacity), f32)
+    for h in range(8):
+        spread = jnp.where(inside & (apart == h * home), one, zero).astype(bf16)
+        stats = stats + jnp.dot(
+            got_ref[h, pl.ds(home, 16), :], spread, preferred_element_type=f32
+        )
+    slot = lax.broadcasted_iota(i32, stats.shape, 1)
+    stats = jnp.where(slot < wide(count, stats.shape), stats, 0.0)
+    for b in range(capacity // ROWS):
+        for m in range(GROUP):
+            lanes = pl.ds(m * ROWS, ROWS)
+            part = stats[:, b * ROWS : (b + 1) * ROWS]
+            stat_ref[0, pl.ds(b, 1), lanes] = part[m : m + 1] * LOG2E
+            stat_ref[1, pl.ds(b, 1), lanes] = part[GROUP + m : GROUP + m + 1]
+    shape = (1024, HEAD_SIZE)
+    lands()
     come = at_owner[...].reshape(1024, HEAD_SIZE)
     told = come.astype(f32).reshape(64, 16, HEAD_SIZE)[:, slots : slots + 1, :]
     told = wide(told, (64, 16, HEAD_SIZE)).reshape(1024, HEAD_SIZE)
@@ -331,15 +358,25 @@
             mine.wait()
         else:
             remote(own_ref, block, z_send.at[d], z_recv.at[d], to_z[d]).wait_recv()
-        for e in (1, 3, 2):
+        for e in (1, 3):
             copy = remote(block, block, x_send.at[d, e], x_recv.at[d, e], to_x[e])
+            copy.start()
+            copies.append(copy)
+    half = BALANCED_TOKENS // 2
+    for d in NEAR_FIRST:
+        source = (z + 8 - d) % 8
+        for e, onward in ((1, 0), (3, 2)):
+            block = kv_ref.at[core, source, (x + 4 - e) % 4]
+            remote(block, block, x_send.at[d, e], x_recv.at[d, e], to_x[e]).wait_recv()
+            part = block.at[pl.ds((onward // 2) * half, half)]
+            copy = remote(part, part, x_send.at[d, onward], x_recv.at[d, onward], to_x[e])
             copy.start()
             copies.append(copy)
     for d in NEAR_FIRST:
         source = (z + 8 - d) % 8
-        for e in (1, 3, 2):
-            block = kv_ref.at[core, source, (x + 4 - e) % 4]
-            remote(block, block, x_send.at[d, e], x_recv.at[d, e], to_x[e]).wait_recv()
+        for onward in (0, 2):
+            part = kv_ref.at[core, source, (x + 2) % 4, pl.ds((onward // 2) * half, half)]
+            remote(part, part, x_send.at[d, onward], x_recv.at[d, onward], to_x[1]).wait_recv()
         row = kv_ref.at[core, source]
         copy = remote(row, row, p_send.at[d], p_recv.at[d], partner)
         copy.start()
@@ -362,12 +399,14 @@
         out_shape=(
             jax.ShapeDtypeStruct((2, 8, 4, BALANCED_TOKENS, 2 * HEAD_SIZE), pack.dtype),
             jax.ShapeDtypeStruct(qd.shape, qd.dtype),
-            jax.ShapeDtypeStruct(pack.shape, pack.dtype),
+            jax.ShapeDtypeStruct((8, HEAD_SIZE), jnp.int32),
+            jax.ShapeDtypeStruct((2, 8, GROUP * ROWS), jnp.float32),
             jax.ShapeDtypeStruct((1024, BALANCED_TOKENS), pack.dtype),
         ),
         in_specs=[vmem, vmem],
-        out_specs=(vmem,) * 4,
+        out_specs=(vmem,) * 5,
         scratch_shapes=[
+            pltpu.VMEM(pack.shape, pack.dtype),
             pltpu.VMEM((64, 16, HEAD_SIZE), pack.dtype),
             pltpu.VMEM((64, 16, HEAD_SIZE), pack.dtype),
             pltpu.VMEM((BALANCED_TOKENS, 2 * HEAD_SIZE), pack.dtype),
@@ -375,7 +414,7 @@
             dma((8,)), dma((8,)), dma((8,)), dma((8,)), dma((64,)), dma((64,)),
         ],
         compiler_params=pltpu.CompilerParams(
-            collective_id=0, has_side_effects=True, vmem_limit_bytes=48 << 20
+            collective_id=0, has_side_effects=True, vmem_limit_bytes=20 << 20
         ),
     )(pack, qd)
 
@@ -452,12 +491,13 @@
         jnp.where(is_key, zero, pick).astype(bf16), part[:, HEAD_SIZE:], preferred_element_type=f32
     )
     to_home[...] = sent.astype(bf16).reshape(64, 16, HEAD_SIZE)
-    drain = scatter_seq(to_home, at_home, own_sem.at[1], s_send, s_recv)
+    lands, drain = scatter_seq(to_home, at_home, own_sem.at[1], s_send, s_recv)
     home = to_slot.shape[1]
     shape = (8 * home, 1024)
     slot = lax.broadcasted_iota(i32, shape, 0)
     column = lax.broadcasted_iota(i32, shape, 1)
     wanted = (((slot & 63) + wide(first_ref[0:1, 0:1], shape)) & 63) * 16 + (slot >> 6)
+    lands()
     come = at_home[...].reshape(1024, HEAD_SIZE)
     for half in range(2):
         chosen = jnp.where(column == wanted + 8 * half, one, zero).astype(bf16)
@@ -505,7 +545,7 @@
             dma((8,)), dma((8,)), dma((8,)), dma((8,)), dma((64,)), dma((64,)),
         ],
         compiler_params=pltpu.CompilerParams(
-            collective_id=1, has_side_effects=True, vmem_limit_bytes=40 << 20
+            collective_id=1, has_side_effects=True, vmem_limit_bytes=24 << 20
         ),
     )(first, pick, dkv, dq)
 
@@ -538,27 +578,16 @@
     first_pack = jnp.concatenate(
         [jnp.concatenate([by_head(keys), by_head(values)], axis=-1), small, digit_rows], axis=1
     )
-    all_kv, qd, first_pack, pick = gather(
+    all_kv, qd, meta, stats, pick = gather(
         first_pack, jnp.concatenate([by_head(queries), by_head(output_gradient)], axis=-1)
     )
-    extra = first_pack[:, home_rows:].astype(jnp.float32)
-    first_rank = (extra[0, 2 * GROUP, 0] * 128 + extra[0, 2 * GROUP, 1]).astype(jnp.int32)
-    count = jnp.sum(extra[:, 2 * GROUP, 2]).astype(jnp.int32)
-
     all_kv = all_kv.reshape(owners, BALANCED_TOKENS, width)
     qd = qd.reshape(capacity, 2 * GROUP * HEAD_SIZE)
 
-    slot = jnp.arange(capacity, dtype=jnp.int32)
-    per_row = extra[:, : 2 * GROUP, :home_rows].transpose(1, 0, 2).reshape(2 * GROUP, capacity)
-    per_row = jnp.where(slot[None, :] < count, per_row, 0.0)
-    per_row = per_row.reshape(2, GROUP, capacity // ROWS, ROWS).transpose(0, 2, 1, 3)
-    per_row = per_row.reshape(2, capacity // ROWS, GROUP * ROWS)
-    dq, dkv = attention(
-        jnp.stack([first_rank, count]), qd, per_row[0] * LOG2E, per_row[1], all_kv
-    )
+    dq, dkv = attention(meta, qd, stats, all_kv)
 
     back, dq = reduce(
-        jnp.broadcast_to(first_rank, (8, HEAD_SIZE)),
+        meta,
         pick,
         dkv.reshape(2, 8, 4, BALANCED_TOKENS, width),
         dq.reshape(heads, home_rows, GROUP * HEAD_SIZE),

time: 171 us -> 155 us (0.906)
  Pallas kernels: 150 us -> 143 us
  local copies, waits for them, and re-layouts: 9.58 us -> 4.65 us
  between operations: 6.02 us -> 4.02 us
  other arithmetic: 5.13 us -> 3.16 us
    unnamed x14 -> x8, local copies, waits for them, and re-layouts: 4.9 us -> 0.67 us
    pallas_call x1, Pallas kernels: 9.6 us -> 5.71 us  [attention(): pl.pallas_call(attention_kernel, name='attention', out_shape=(jax.ShapeDt...]
    pallas_call x1, Pallas kernels: 68.7 us -> 66.1 us  [gather(): pl.pallas_call(gather_kernel, name='gather', out_shape=(jax.ShapeDtypeStr...]
where the time goes in v4:
time: 155 us; the launch traced here: 154 us
  Pallas kernels  143 us (92%)
  local copies, waits for them, and re-layouts  4.65 us (3%)
  between operations  4.02 us (3%)
  other arithmetic  3.16 us (2%)
    pallas_call x1, Pallas kernels, reduce(): pl.pallas_call(reduce_kernel, name='reduce', out_shape=(jax.ShapeDtypeStr...  70.8 us
    pallas_call x1, Pallas kernels, gather(): pl.pallas_call(gather_kernel, name='gather', out_shape=(jax.ShapeDtypeStr...  66.1 us
    pallas_call x1, Pallas kernels, attention(): pl.pallas_call(attention_kernel, name='attention', out_shape=(jax.ShapeDt...  5.71 us

profile of v4, /device:TPU:1, one launch (start us, length us, event | category | flops | bytes accessed | tf_op | source)
XLA Modules:
  0.0 154.4 jit_solution(12250387955100310695)
XLA Ops:
  0.6 0.0 copy-start
  0.6 1.3 fusion.9
  5.2 0.1 fusion.8
  5.3 0.7 reshape.51
  6.1 0.0 copy-done
  6.1 0.9 bitcast_bitcast_fusion.2
  7.0 1.3 multiply_bitcast_fusion
  8.3 0.0 copy-start.1
  8.3 0.0 copy-start.2
  8.3 0.2 copy.40
  8.5 0.3 reduce_sum.18
  8.8 0.1 copy.27
  9.0 0.3 copy-done.1
  9.3 0.1 copy-done.2
  9.5 0.1 bitcast_bitcast_fusion
  9.5 0.1 pad_maximum_fusion.qd_ref
  9.6 66.1 %gather.1 = (bf16[2,8,4,128,256]{4,3,2,1,0:T(8,128)(2,1)S(1)}, bf16[8,48,1280]{2,1,0:T(8,128)(2,1)S(1)}, s32[8,128]{1,0:T(8,128)S(1)}, f32[2,8,640]{2,1,0:T(8,128)S(1)}, bf16[1024,128]{1,0:T(8,128)(2,1)S(1)}) custom-call(bf16[8,64,256]{2,1,0:T(8,128)(2,1)S(1)} %fusion.3.pack_ref, bf16[8,48,1280]{2,1,0:T(8,128)(2,1)S(1)} %pad_maximum_fusion.qd_ref), custom_call_target="tpu_custom_call" | custom-call | tf_op jit(solution)/shard_map/gather/pallas_call | solution.py:396
  75.7 5.7 %attention.1 = (bf16[384,640]{1,0:T(8,128)(2,1)S(1)}, bf16[64,128,256]{2,1,0:T(8,128)(2,1)S(1)}) custom-call(s32[8,128]{1,0:T(8,128)S(1)} %get-tuple-element.12.meta_ref.first_ref, bf16[384,1280]{1,0:T(8,128)(2,1)S(1)} %bitcast.63, f32[2,8,640]{2,1,0:T(8,128)S(1)} %get-tuple-element.15.stat_ref, bf16[64,128,256]{2,1,0:T(8,128)(2,1)S(1)} %bitcast.62), custom_call_target="tpu_custom_call" | custom-call | flops 10066329600 | bytes 11337728 | tf_op jit(solution)/shard_map/attention/pallas_call | solution.py:109
  81.5 70.8 %reduce.1 = (bf16[8,48,256]{2,1,0:T(8,128)(2,1)S(1)}, bf16[8,48,640]{2,1,0:T(8,128)(2,1)S(1)}) custom-call(s32[8,128]{1,0:T(8,128)S(1)} %get-tuple-element.12.meta_ref.first_ref, bf16[1024,128]{1,0:T(8,128)(2,1)S(1)} %get-tuple-element.13.pick_ref, bf16[2,8,4,128,256]{4,3,2,1,0:T(8,128)(2,1)S(1)} %bitcast.59, bf16[8,48,640]{2,1,0:T(8,128)(2,1)S(1)} %bitcast.61), custom_call_target="tpu_custom_call" | custom-call | tf_op jit(solution)/shard_map/reduce/pallas_call | solution.py:525
  152.3 0.8 copy.37
  153.1 0.7 copy.47
  153.8 0.7 copy.48
  (5 shorter events, 0.1 us)
Async XLA Ops:
  0.6 5.4 %copy-start = (bf16[48,1024]{1,0:T(8,128)(2,1)S(1)}, bf16[48,1024]{1,0:T(8,128)(2,1)}, u32[]{:S(2)}) copy-start(bf16[48,1024]{1,0:T(8,128)(2,1)} %param.8) | copy-start | bytes 294916
  8.3 1.0 copy-start.1
  8.3 1.2 copy-start.2
